TPU v7x, 512 devices: a whole 4x8x8 slice. The times are simulated.
512 devices in a mesh: region: 32 (over x, y), shard: 16 (over z, core).
Axes of the slice: x: 4, y: 8, z: 8, core: 2. Of those that a mesh axis runs over, the one named last changes fastest.
Arguments:
- state_anom: float32 [524288, 256], P(('region', 'shard')), may hold values from -6 to 6
- state_mean: float32 [524288], P(('region', 'shard')), may hold values from -6 to 6
- obs_anom: float32 [64, 512, 256], P('region', 'shard'), may hold values from -6 to 6
- obs_depart: float32 [64, 512], P('region', 'shard'), may hold values from -6 to 6
- obs_var: float32 [64, 512], P('region', 'shard'), may hold values from 0.5 to 2
- taper_levels: float32 [8], replicated, may hold values from 0 to 1
- state_taper: int32 [4096, 256], P(('region', 'shard')), may hold values from 0 to 7
- obs_taper: int32 [256, 256], P('region'), may hold values from 0 to 7
- batch_order: int32 [3], replicated, may hold values from 0 to 63, as said below
Outputs:
- post_anom: float32 [524288, 256], P(('region', 'shard'))
- post_mean: float32 [524288], P(('region', 'shard'))
- post_obs_anom: float32 [64, 512, 256], P('region', 'shard')
- post_obs_depart: float32 [64, 512], P('region', 'shard')
Inputs may be any that keep to these rules, and one draw needn't show every extreme that they name: `batch_order`: 3 distinct batch numbers; batch q lies in region q // 2; the first and the last batch number both occur.
All inputs are finite; a program needn't handle non-finite values.
Results may differ from a plain program's by a relative error of at most 0.0001.
Values sent between devices are 32-bit elements; how exact they have to be, the bound alone decides.
No kernel may reach another device: no remote copies, remote signals or barrier semaphores. Data moves between devices by JAX's collectives and lax.ppermute only.
A program may use at most 64 MiB of HBM per device.

v0:
```python
import jax
import jax.numpy as jnp
from jax import lax
from jax.experimental import pallas as pl
from jax.experimental.pallas import tpu as pltpu
from jax.sharding import Mesh, PartitionSpec as P

M = 256
N = 512
B = 128
NBLK = N // B
NB = 3
KB = 2
XS, YS, ZS, CS = 4, 8, 8, 2
PIECE = 32
WIDE = M + B
HI = lax.Precision.HIGHEST
F32 = jnp.float32


def mm(a, b, ca=1, cb=0):
    return lax.dot_general(a, b, (((ca,), (cb,)), ((), ())), precision=HI, preferred_element_type=F32)


def iota(shape, axis):
    return lax.broadcasted_iota(jnp.int32, shape, axis)


def wide(v):
    return jnp.concatenate([v, v], axis=1)


def split(v):
    hi = v.astype(jnp.bfloat16)
    rest = v - hi.astype(F32)
    mid = rest.astype(jnp.bfloat16)
    return hi, mid, (rest - mid.astype(F32)).astype(jnp.bfloat16)


def factor_block(a_ref, p_ref, w_ref):
    groups = B // 8
    rows = [jnp.broadcast_to(a_ref[s : s + 1, :], (8, 2 * B)) for s in range(8)]
    for g in range(groups):
        j0 = 8 * g
        d = {}
        for s in range(8):
            for t in range(s + 1):
                d[s, t] = jnp.broadcast_to(rows[t][:, j0 + s : j0 + s + 1], (8, B))
        if g < groups - 1:
            ahead = [jnp.broadcast_to(a_ref[j0 + 8 + s : j0 + 9 + s, :], (8, 2 * B)) for s in range(8)]
        low = {}
        for t in range(8):
            inv = lax.rsqrt(d[t, t])
            done = rows[t] * wide(inv)
            for s in range(t + 1, 8):
                low[s, t] = d[s, t] * inv
            for s in range(t + 1, 8):
                for v in range(t + 1, s + 1):
                    d[s, v] = d[s, v] - low[s, t] * low[v, t]
            for s in range(t + 1, 8):
                rows[s] = rows[s] - wide(low[s, t]) * done
            w_ref[j0 + t : j0 + t + 1, :] = done[:1, B:]
            if g < groups - 1:
                p_ref[j0 + t : j0 + t + 1, :] = done[:1, :]
                for s in range(8):
                    ahead[s] = ahead[s] - wide(jnp.broadcast_to(done[:, j0 + 8 + s : j0 + 9 + s], (8, B))) * done
        if g == groups - 1:
            break
        rows = ahead
        lo = j0 + 16
        if lo < B:
            hi, mid, rest = split(p_ref[j0 : j0 + 8, :])
            left = jnp.concatenate([hi, hi, hi, mid, mid, rest])[:, :B]
            right = jnp.concatenate([hi, mid, rest, hi, mid, hi])
            fix = lax.dot_general(left, right, (((0,), (0,)), ((), ())), preferred_element_type=F32)
            a_ref[lo:, :] = a_ref[lo:, :] - fix[lo:, :]

def lower_inverses(ts):
    ri, ci = iota((B, B), 0), iota((B, B), 1)
    xs = [jnp.where(ri == ci, 1.0 / t, 0.0) for t in ts]
    m = 1
    while m < B:
        mask = (ri // (2 * m) == ci // (2 * m)) & ((ri // m) % 2 == 1) & ((ci // m) % 2 == 0)
        mid = [mm(jnp.where(mask, t, 0.0), x) for t, x in zip(ts, xs)]
        xs = [x - mm(x, y) for x, y in zip(xs, mid)]
        m *= 2
    return xs


def analysis_kernel(
    order_ref, levels_ref, stape_ref, otape_ref, mine_ref, one_ref, two_ref, x_ref, mean_ref, obs_ref,
    xo_ref, meano_ref, obso_ref, depo_ref,
    y_ref, d_ref, r_ref, c_ref, s_ref, u_ref, w_ref, a_ref, p_ref, v_ref, g_ref, dm_ref, do_ref,
):
    eye = iota((B, B), 0) == iota((B, B), 1)
    low_mask = iota((B, B), 0) >= iota((B, B), 1)
    piece_eye = iota((PIECE, B), 0) == iota((PIECE, B), 1)
    var_eye = iota((PIECE, B), 0) + PIECE == iota((PIECE, B), 1)
    pairs = NB * NBLK * NBLK
    pair_eye = iota((pairs, B), 0) + 2 * PIECE == iota((pairs, B), 1)

    def column(line, mask):
        col = jnp.sum(jnp.where(mask, line, 0.0), axis=1, keepdims=True)
        return jnp.broadcast_to(col, mask.shape)

    def unpack(s, carry):
        at = pl.multiple_of(s * PIECE, PIECE)
        y_ref[0, pl.ds(at, 32), :] = one_ref[s, 0:32, :]
        y_ref[1, pl.ds(at, 32), :] = two_ref[s, 0:32, :]
        y_ref[2, pl.ds(at, 24), :] = two_ref[s, 32:56, :]
        y_ref[2, pl.ds(at + 24, 8), :] = one_ref[s, 40:48, :]
        for k in range(NB):
            line = one_ref[s, 32 + k : 33 + k, :B]
            d_ref[k, pl.ds(at, PIECE), :] = column(line, piece_eye)
            r_ref[k, pl.ds(at, PIECE), :] = column(line, var_eye)
        return carry

    lax.fori_loop(0, ZS * CS, unpack, 0)
    for k in range(NB):
        c_ref[k * pairs : k * pairs + pairs, :] = column(one_ref[0, 32 + k : 33 + k, :B], pair_eye)
    xo_ref[...] = x_ref[...]
    obso_ref[...] = obs_ref[...]
    dm_ref[...] = jnp.zeros_like(dm_ref)
    do_ref[...] = jnp.zeros_like(do_ref)

    def batch_step(k, outer):
        s_ref[:, :N] = mm(y_ref[k], y_ref[k], 1, 1) * (1.0 / (M - 1))
        s_ref[:, N:] = d_ref[k]
        for b in range(NBLK):
            sl = slice(b * B, b * B + B)
            s_ref[sl, sl] = s_ref[sl, sl] + jnp.where(eye, r_ref[k, sl, :], 0.0)

        def block_step(b, carry):
            at = pl.multiple_of(b * B, B)
            a_ref[:, :B] = s_ref[pl.ds(at, B), pl.ds(at, B)]
            a_ref[:, B:] = jnp.where(eye, 1.0, 0.0)
            factor_block(a_ref, p_ref, w_ref.at[b])
            inv = w_ref[b]
            row = mm(inv, s_ref[pl.ds(at, B), :])
            u_ref[pl.ds(at, B), :] = row
            for c in range(NBLK - 1):
                @pl.when(b == c)
                def _():
                    lo = (c + 1) * B
                    q = mm(inv, u_ref[lo - B : lo, lo:], 0, 0)
                    s_ref[lo:, lo:] = s_ref[lo:, lo:] - mm(s_ref[lo:, lo - B : lo], q)
            return carry

        lax.fori_loop(0, NBLK, block_step, 0)

        shifted = []
        for b in range(NBLK):
            sl = slice(b * B, b * B + B)
            low = jnp.where(low_mask, jnp.transpose(u_ref[sl, sl]), 0.0)
            shifted.append(low + jnp.where(eye, jnp.sqrt(r_ref[k, sl, :]), 0.0))
        tinv = lower_inverses(shifted)

        v_ref[:, :M] = y_ref[k]
        v_ref[:, M:] = u_ref[:, N:]
        for b in range(NBLK):
            sl = slice(b * B, b * B + B)
            hi = (b + 1) * B
            v_ref[sl, :M] = mm(tinv[b], v_ref[sl, :M])
            if b < NBLK - 1:
                v_ref[hi:, :M] = v_ref[hi:, :M] - mm(u_ref[sl, hi:N], v_ref[sl, :M], 0, 0)
        for b in range(NBLK - 1, -1, -1):
            sl = slice(b * B, b * B + B)
            hi = (b + 1) * B
            rhs = v_ref[sl, :]
            if b < NBLK - 1:
                rhs = rhs - mm(u_ref[sl, hi:N], v_ref[hi:, :])
            v_ref[sl, :] = mm(w_ref[b], rhs, 0, 0)
        for b in range(NBLK):
            sl = slice(b * B, b * B + B)
            g_ref[b] = mm(y_ref[k, sl, :], v_ref[sl, :], 0, 0) * (1.0 / (M - 1))

        def gain(weight):
            total = weight(0) * g_ref[0]
            for j in range(1, NBLK):
                total = total + weight(j) * g_ref[j]
            return total

        def cross_step(n, carry):
            later, i = n // NBLK, n % NBLK
            at = pl.multiple_of(i * B, B)

            def weight(j):
                line = c_ref[pl.ds(later * pairs + k * (NBLK * NBLK) + i * NBLK + j, 1), :]
                return jnp.concatenate([line] * (WIDE // B), axis=1)

            delta = mm(y_ref[later, pl.ds(at, B), :], gain(weight))
            y_ref[later, pl.ds(at, B), :] = y_ref[later, pl.ds(at, B), :] - delta[:, :M]
            d_ref[later, pl.ds(at, B), :] = d_ref[later, pl.ds(at, B), :] - delta[:, M:]
            return carry

        lax.fori_loop((k + 1) * NBLK, NB * NBLK, cross_step, 0)
        first = order_ref[k] * NBLK

        def state_step(i, carry):
            at = pl.multiple_of(i * B, B)
            rows = xo_ref[pl.ds(at, B), :]
            delta = mm(rows, gain(lambda j: levels_ref[stape_ref[i, first + j]]))
            xo_ref[pl.ds(at, B), :] = rows - delta[:, :M]
            dm_ref[pl.ds(at, B), :] = dm_ref[pl.ds(at, B), :] + delta[:, M:]
            return carry

        lax.fori_loop(0, x_ref.shape[0] // B, state_step, 0)
        for q in range(KB):
            sl = slice(q * PIECE, q * PIECE + PIECE)
            rows = obso_ref[sl, :]
            delta = mm(rows, gain(lambda j: levels_ref[otape_ref[q * NBLK + mine_ref[0], first + j]]))
            obso_ref[sl, :] = rows - delta[:, :M]
            do_ref[sl, :] = do_ref[sl, :] + delta[:, M:]
        return outer

    lax.fori_loop(0, NB, batch_step, 0)

    for i in range(x_ref.shape[0] // B):
        sl = slice(i * B, i * B + B)
        add = jnp.sum(jnp.where(eye, dm_ref[sl, :], 0.0), axis=0, keepdims=True)
        meano_ref[i : i + 1, :] = mean_ref[i : i + 1, :] + add
    for q in range(KB):
        sl = slice(q * PIECE, q * PIECE + PIECE)
        sub = jnp.sum(jnp.where(piece_eye, do_ref[sl, :], 0.0), axis=0, keepdims=True)
        depo_ref[q : q + 1, :] = sub


def analysis(order, levels, stape, otape, mine, one, two, x, mean, obs):
    shape = lambda *dims: jax.ShapeDtypeStruct(dims, F32)
    scratch = lambda *dims: pltpu.VMEM(dims, F32)
    vmem = pl.BlockSpec(memory_space=pltpu.VMEM)
    rows = x.shape[0]
    return pl.pallas_call(
        analysis_kernel,
        out_shape=[shape(rows, M), shape(rows // B, B), shape(KB * PIECE, M), shape(KB, B)],
        in_specs=[pl.BlockSpec(memory_space=pltpu.SMEM)] * 5 + [vmem] * 5,
        out_specs=[vmem] * 4,
        scratch_shapes=[
            scratch(NB, N, M),
            scratch(NB, N, B),
            scratch(NB, N, B),
            scratch(NB * NB * NBLK * NBLK, B),
            scratch(N, N + B),
            scratch(N, N + B),
            scratch(NBLK, B, B),
            scratch(B, 2 * B),
            scratch(B, 2 * B),
            scratch(N, WIDE),
            scratch(NBLK, M, WIDE),
            scratch(rows, B),
            scratch(KB * PIECE, B),
        ],
        name="analysis",
    )(order, levels, stape, otape, mine, one, two, x, mean, obs)


ROWS = 104


def prepare_kernel(order_ref, levels_ref, otape_ref, obs_ref, dep_ref, var_ref, out_ref):
    local = [order_ref[k] % KB for k in range(NB)]
    out_ref[0:32, :] = obs_ref[local[0]]
    out_ref[48:80, :] = obs_ref[local[1]]
    out_ref[80:104, :] = obs_ref[local[2], 0:24, :]
    out_ref[40:48, :] = obs_ref[local[2], 24:32, :]
    out_ref[32:40, :] = jnp.zeros((8, M), F32)
    lane = iota((1, B), 1)
    for k in range(NB):
        line = jnp.zeros((1, B), F32)
        for b in range(NB):
            for i in range(NBLK):
                for j in range(NBLK):
                    weight = levels_ref[otape_ref[local[k] * NBLK + i, order_ref[b] * NBLK + j]]
                    line = jnp.where(lane == 2 * PIECE + (b * NBLK + i) * NBLK + j, weight, line)
        out_ref[32 + k : 33 + k, :B] = line
        for q in range(KB):
            @pl.when(local[k] == q)
            def _():
                out_ref[32 + k : 33 + k, 0:PIECE] = dep_ref[q : q + 1, :]
                out_ref[32 + k : 33 + k, PIECE : 2 * PIECE] = var_ref[q : q + 1, :]


def prepare(order, levels, otape, obs, dep, var):
    vmem = pl.BlockSpec(memory_space=pltpu.VMEM)
    return pl.pallas_call(
        prepare_kernel,
        out_shape=jax.ShapeDtypeStruct((ROWS, M), F32),
        in_specs=[pl.BlockSpec(memory_space=pltpu.SMEM)] * 3 + [vmem] * 3,
        out_specs=vmem,
        name="prepare",
    )(order, levels, otape, obs, dep, var)


def spread(block, roots, axis, size):
    place = lax.axis_index(axis)
    away = [(place - roots[k] + size) % size for k in range(NB)]
    row = iota(block.shape, 0)
    second = (row == 33) | ((row >= 48) & (row < 80))
    third = (row == 34) | ((row >= 40) & (row < 48)) | (row >= 80)
    far = jnp.where(second, away[1], jnp.where(third, away[2], away[0]))
    step = size // 2
    while step:
        moved = lax.ppermute(block, axis, [(i, (i + step) % size) for i in range(size)])
        block = jnp.where(far % (2 * step) == 0, block, moved)
        step //= 2
    return block


def per_device(state_anom, state_mean, obs_anom, obs_depart, obs_var, taper_levels, state_taper, obs_taper, batch_order):
    shard = lax.axis_index("z") * CS + lax.axis_index("c")
    owner = batch_order // KB
    payload = prepare(batch_order, taper_levels, obs_taper, obs_anom, obs_depart, obs_var)
    payload = spread(payload, owner // YS, "x", XS)
    payload = spread(payload, owner % YS, "y", YS)
    one = lax.all_gather(payload[:48], ("z", "c"))
    two = lax.all_gather(payload[48:], ("z", "c"))
    mine = (shard * PIECE // B).astype(jnp.int32).reshape(1)
    rows = state_anom.shape[0]
    anomaly, mean, obs_now, moved = analysis(
        batch_order, taper_levels, state_taper, obs_taper, mine, one, two,
        state_anom, state_mean.reshape(rows // B, B), obs_anom.reshape(KB * PIECE, M),
    )
    return (
        anomaly,
        mean.reshape(rows),
        obs_now.reshape(obs_anom.shape),
        obs_depart - moved[:, :PIECE],
    )


def solution(mesh):
    fine = Mesh(mesh.devices.reshape(XS, YS, ZS, CS), ("x", "y", "z", "c")) if hasattr(mesh, "devices") else mesh
    region, shard, both = ("x", "y"), ("z", "c"), ("x", "y", "z", "c")
    placed = (
        P(both, None),
        P(both),
        P(region, shard, None),
        P(region, shard),
        P(region, shard),
        P(),
        P(both, None),
        P(region, None),
        P(),
    )
    return jax.shard_map(
        per_device,
        mesh=fine,
        in_specs=placed,
        out_specs=(P(both, None), P(both), P(region, shard, None), P(region, shard)),
        check_vma=False,
    )
```

profile of v0, /device:TPU:1, one launch (start us, length us, event | category | flops | bytes accessed | tf_op | source)
XLA Modules:
  0.0 213.2 jit_solution(4493180713471423734)
XLA Ops:
  0.6 0.0 copy-start.2
  0.6 2.1 prepare.1
  2.7 0.0 copy-start
  2.7 5.6 %collective-permute-start = (f32[104,256]{1,0:T(8,128)}, f32[104,256]{1,0:T(8,128)S(1)}, u32[]{:S(2)}, u32[]{:S(2)}) collective-permute-start(f32[104,256]{1,0:T(8,128)} %prepare.1), channel_id=1, source_target_pairs={{0,256},{128,384},{256,0},{384,128},{1,257},{129,385},{257,1},{385... | collective-permute-start | bytes 319496 | tf_op jit(solution)/shard_map/ppermute | solution.py:303
  8.3 0.0 copy-done.2
  8.4 0.6 fusion.16
  11.0 0.0 collective-permute-done
  11.0 0.0 copy-done
  11.0 0.1 fusion.10
  11.1 3.2 %collective-permute-start.1 = (f32[104,256]{1,0:T(8,128)S(1)}, f32[104,256]{1,0:T(8,128)S(1)}, u32[]{:S(2)}, u32[]{:S(2)}) collective-permute-start(f32[104,256]{1,0:T(8,128)S(1)} %fusion.10), channel_id=1, source_target_pairs={{0,128},{128,256},{256,384},{384,0},{1,129},{129,257},{257,385},{3... | collective-permute-start | bytes 319496 | tf_op jit(solution)/shard_map/ppermute | solution.py:303
  14.4 0.6 fusion.15
  16.9 1.5 collective-permute-done.1
  18.4 0.1 fusion.11
  18.5 6.9 %collective-permute-start.2 = (f32[104,256]{1,0:T(8,128)S(1)}, f32[104,256]{1,0:T(8,128)S(1)}, u32[]{:S(2)}, u32[]{:S(2)}) collective-permute-start(f32[104,256]{1,0:T(8,128)S(1)} %fusion.11), channel_id=1, source_target_pairs={{0,64},{16,80},{32,96},{48,112},{64,0},{80,16},{96,32},{112,48},{1... | collective-permute-start | bytes 319496 | tf_op jit(solution)/shard_map/ppermute | solution.py:303
  25.5 2.5 %collective-permute-done.2 = f32[104,256]{1,0:T(8,128)S(1)} collective-permute-done((f32[104,256]{1,0:T(8,128)S(1)}, f32[104,256]{1,0:T(8,128)S(1)}, u32[]{:S(2)}, u32[]{:S(2)}) %collective-permute-start.2) | collective-permute-done | bytes 106528 | tf_op jit(solution)/shard_map/ppermute | solution.py:303
  28.0 0.1 fusion.12
  28.1 4.7 %collective-permute-start.3 = (f32[104,256]{1,0:T(8,128)S(1)}, f32[104,256]{1,0:T(8,128)S(1)}, u32[]{:S(2)}, u32[]{:S(2)}) collective-permute-start(f32[104,256]{1,0:T(8,128)S(1)} %fusion.12), channel_id=1, source_target_pairs={{0,32},{16,48},{32,64},{48,80},{64,96},{80,112},{96,0},{112,16},{1... | collective-permute-start | bytes 319496 | tf_op jit(solution)/shard_map/ppermute | solution.py:303
  32.8 4.1 %collective-permute-done.3 = f32[104,256]{1,0:T(8,128)S(1)} collective-permute-done((f32[104,256]{1,0:T(8,128)S(1)}, f32[104,256]{1,0:T(8,128)S(1)}, u32[]{:S(2)}, u32[]{:S(2)}) %collective-permute-start.3) | collective-permute-done | bytes 106528 | tf_op jit(solution)/shard_map/ppermute | solution.py:303
  36.9 0.1 fusion.13
  37.0 4.1 %collective-permute-start.4 = (f32[104,256]{1,0:T(8,128)S(1)}, f32[104,256]{1,0:T(8,128)S(1)}, u32[]{:S(2)}, u32[]{:S(2)}) collective-permute-start(f32[104,256]{1,0:T(8,128)S(1)} %fusion.13), channel_id=1, source_target_pairs={{0,16},{16,32},{32,48},{48,64},{64,80},{80,96},{96,112},{112,0},{1... | collective-permute-start | bytes 319496 | tf_op jit(solution)/shard_map/ppermute | solution.py:303
  41.2 2.5 %collective-permute-done.4 = f32[104,256]{1,0:T(8,128)S(1)} collective-permute-done((f32[104,256]{1,0:T(8,128)S(1)}, f32[104,256]{1,0:T(8,128)S(1)}, u32[]{:S(2)}, u32[]{:S(2)}) %collective-permute-start.4) | collective-permute-done | bytes 106528 | tf_op jit(solution)/shard_map/ppermute | solution.py:303
  43.7 0.1 fusion.14
  43.8 32.2 %all-gather = f32[768,256]{1,0:T(8,128)} all-gather(f32[48,256]{1,0:T(8,128)S(1)} %slice.36), channel_id=2, replica_groups=mesh['x'=4,'y'=8,'z'=8,'c'=2] {'z','c'}, dimensions={0}, use_global_device_ids=true | all-gather | bytes 835584 | tf_op jit(solution)/shard_map/all_gather | solution.py:315
  76.1 18.5 %all-gather.1 = f32[896,256]{1,0:T(8,128)} all-gather(f32[56,256]{1,0:T(8,128)S(1)} %slice.37), channel_id=3, replica_groups=mesh['x'=4,'y'=8,'z'=8,'c'=2] {'z','c'}, dimensions={0}, use_global_device_ids=true | all-gather | bytes 974848 | tf_op jit(solution)/shard_map/all_gather | solution.py:316
  94.5 116.8 %analysis.1 = (f32[1024,256]{1,0:T(8,128)}, f32[8,128]{1,0:T(8,128)}, f32[64,256]{1,0:T(8,128)}, f32[2,128]{1,0:T(2,128)}) custom-call(s32[3]{0:T(128)} %order_ref.3, f32[8]{0:T(128)} %levels_ref.3, s32[8,256]{1,0:T(8,128)} %stape_ref.1, s32[8,256]{1,0:T(8,128)} %otape_ref.3, s32[1]{0:T(128)} %bitcast.mine_ref, f32[16,48,256]{2,1,0:T(8,128)} %bitcast.14, ...), custom_call_target="tpu_custom_call" | custom-call | tf_op jit(solution)/shard_map/analysis/pallas_call | solution.py:233
  211.3 0.0 copy-start.1
  211.3 0.7 copy-done.1
  212.0 1.2 slice_subtract_fusion
  (7 shorter events, 0.1 us)
Async XLA Ops:
  0.6 7.7 %copy-start.2 = (s32[3]{0:T(128)S(1)}, s32[3]{0:T(128)}, u32[]{:S(2)}) copy-start(s32[3]{0:T(128)} %order_ref.3) | copy-start | bytes 40
  2.7 8.3 %copy-start = (f32[104,256]{1,0:T(8,128)S(1)}, f32[104,256]{1,0:T(8,128)}, u32[]{:S(2)}) copy-start(f32[104,256]{1,0:T(8,128)} %prepare.1) | copy-start | bytes 319492
  2.7 8.3 %collective-permute-start = (f32[104,256]{1,0:T(8,128)}, f32[104,256]{1,0:T(8,128)S(1)}, u32[]{:S(2)}, u32[]{:S(2)}) collective-permute-start(f32[104,256]{1,0:T(8,128)} %prepare.1), channel_id=1, source_target_pairs={{0,256},{128,384},{256,0},{384,128},{1,257},{129,385},{257,1},{385... | collective-permute-start | bytes 319496 | tf_op jit(solution)/shard_map/ppermute | solution.py:303
  11.1 7.3 %collective-permute-start.1 = (f32[104,256]{1,0:T(8,128)S(1)}, f32[104,256]{1,0:T(8,128)S(1)}, u32[]{:S(2)}, u32[]{:S(2)}) collective-permute-start(f32[104,256]{1,0:T(8,128)S(1)} %fusion.10), channel_id=1, source_target_pairs={{0,128},{128,256},{256,384},{384,0},{1,129},{129,257},{257,385},{3... | collective-permute-start | bytes 319496 | tf_op jit(solution)/shard_map/ppermute | solution.py:303
  18.5 9.5 %collective-permute-start.2 = (f32[104,256]{1,0:T(8,128)S(1)}, f32[104,256]{1,0:T(8,128)S(1)}, u32[]{:S(2)}, u32[]{:S(2)}) collective-permute-start(f32[104,256]{1,0:T(8,128)S(1)} %fusion.11), channel_id=1, source_target_pairs={{0,64},{16,80},{32,96},{48,112},{64,0},{80,16},{96,32},{112,48},{1... | collective-permute-start | bytes 319496 | tf_op jit(solution)/shard_map/ppermute | solution.py:303
  28.1 8.8 %collective-permute-start.3 = (f32[104,256]{1,0:T(8,128)S(1)}, f32[104,256]{1,0:T(8,128)S(1)}, u32[]{:S(2)}, u32[]{:S(2)}) collective-permute-start(f32[104,256]{1,0:T(8,128)S(1)} %fusion.12), channel_id=1, source_target_pairs={{0,32},{16,48},{32,64},{48,80},{64,96},{80,112},{96,0},{112,16},{1... | collective-permute-start | bytes 319496 | tf_op jit(solution)/shard_map/ppermute | solution.py:303
  37.0 6.7 %collective-permute-start.4 = (f32[104,256]{1,0:T(8,128)S(1)}, f32[104,256]{1,0:T(8,128)S(1)}, u32[]{:S(2)}, u32[]{:S(2)}) collective-permute-start(f32[104,256]{1,0:T(8,128)S(1)} %fusion.13), channel_id=1, source_target_pairs={{0,16},{16,32},{32,48},{48,64},{64,80},{80,96},{96,112},{112,0},{1... | collective-permute-start | bytes 319496 | tf_op jit(solution)/shard_map/ppermute | solution.py:303
  211.3 0.7 copy-start.1
where the time goes:
time: 214 us; the launch traced here: 213 us
  Pallas kernels  119 us (56%)
  blocking collectives  50.7 us (24%)
  starting transfers between devices  24.6 us (11%)
  waiting for transfers between devices  10.6 us (5%)
  between operations  4.81 us (2%)
    pallas_call x1, Pallas kernels, analysis(): pl.pallas_call(analysis_kernel, out_shape=[shape(rows, M), shape(rows //...  117 us
    all_gather x1, blocking collectives, per_device(): one = lax.all_gather(payload[:48], ('z', 'c'))  32.2 us
    ppermute x5, starting transfers between devices, spread(): lax.ppermute(block, axis, [(i, (i + step) % size) for i in range(size)])  24.6 us
    all_gather x1, blocking collectives, per_device(): two = lax.all_gather(payload[48:], ('z', 'c'))  18.5 us
    ppermute x5, waiting for transfers between devices, spread(): lax.ppermute(block, axis, [(i, (i + step) % size) for i in range(size)])  10.6 us
  transfers between devices with their start and end apart: 5, of which 4 were waited for; matrix products, arithmetic and copies ran while one was open for 1% of the time, Pallas kernels for 0%

commit v1 on v0

--- a/solution.py
+++ b/solution.py
@@ -22,6 +22,17 @@
     return lax.dot_general(a, b, (((ca,), (cb,)), ((), ())), precision=HI, preferred_element_type=F32)
 
 
+def halves(v):
+    hi = v.astype(jnp.bfloat16)
+    return hi, (v - hi.astype(F32)).astype(jnp.bfloat16)
+
+
+def mm3(a, b, ca=1, cb=0):
+    dot = lambda p, q: lax.dot_general(p, q, (((ca,), (cb,)), ((), ())), preferred_element_type=F32)
+    (ah, al), (bh, bl) = halves(a), halves(b)
+    return dot(ah, bh) + (dot(ah, bl) + dot(al, bh))
+
+
 def iota(shape, axis):
     return lax.broadcasted_iota(jnp.int32, shape, axis)
 
@@ -37,8 +48,9 @@
     return hi, mid, (rest - mid.astype(F32)).astype(jnp.bfloat16)
 
 
-def factor_block(a_ref, p_ref, w_ref):
+def factor_block(a_ref, p_ref, w_ref, root_ref, base_ref, hooks):
     groups = B // 8
+    lane = iota((8, B), 1)
     rows = [jnp.broadcast_to(a_ref[s : s + 1, :], (8, 2 * B)) for s in range(8)]
     for g in range(groups):
         j0 = 8 * g
@@ -48,9 +60,10 @@
                 d[s, t] = jnp.broadcast_to(rows[t][:, j0 + s : j0 + s + 1], (8, B))
         if g < groups - 1:
             ahead = [jnp.broadcast_to(a_ref[j0 + 8 + s : j0 + 9 + s, :], (8, 2 * B)) for s in range(8)]
-        low = {}
+        low, diag = {}, []
         for t in range(8):
             inv = lax.rsqrt(d[t, t])
+            diag.append(d[t, t] * inv)
             done = rows[t] * wide(inv)
             for s in range(t + 1, 8):
                 low[s, t] = d[s, t] * inv
@@ -64,6 +77,16 @@
                 p_ref[j0 + t : j0 + t + 1, :] = done[:1, :]
                 for s in range(8):
                     ahead[s] = ahead[s] - wide(jnp.broadcast_to(done[:, j0 + 8 + s : j0 + 9 + s], (8, B))) * done
+        small = []
+        for s in range(8):
+            row = jnp.where(lane == j0 + s, 1.0, 0.0)
+            for t in range(s):
+                row = row - low[s, t] * small[t]
+            shift = jnp.broadcast_to(root_ref[j0 + s : j0 + s + 1, :], (8, B))
+            small.append(row * (1.0 / (diag[s] + shift)))
+            base_ref[j0 + s : j0 + s + 1, :] = small[s][:1, :]
+        if hooks.get(g):
+            hooks[g]()
         if g == groups - 1:
             break
         rows = ahead
@@ -75,25 +98,34 @@
             fix = lax.dot_general(left, right, (((0,), (0,)), ((), ())), preferred_element_type=F32)
             a_ref[lo:, :] = a_ref[lo:, :] - fix[lo:, :]
 
-def lower_inverses(ts):
+def doubling_steps(u, low_ref, x_ref, mid_ref):
     ri, ci = iota((B, B), 0), iota((B, B), 1)
-    xs = [jnp.where(ri == ci, 1.0 / t, 0.0) for t in ts]
-    m = 1
-    while m < B:
+
+    def first():
+        low_ref[...] = jnp.transpose(u())
+
+    def half(m):
         mask = (ri // (2 * m) == ci // (2 * m)) & ((ri // m) % 2 == 1) & ((ci // m) % 2 == 0)
-        mid = [mm(jnp.where(mask, t, 0.0), x) for t, x in zip(ts, xs)]
-        xs = [x - mm(x, y) for x, y in zip(xs, mid)]
-        m *= 2
-    return xs
+        mid_ref[...] = mm(jnp.where(mask, low_ref[...], 0.0), x_ref[...])
+
+    def full():
+        x_ref[...] = x_ref[...] - mm(x_ref[...], mid_ref[...])
+
+    steps = [first]
+    for m in (8, 16, 32, 64):
+        steps += [lambda m=m: half(m), full]
+    return steps
+
+
+BASE = NBLK
 
 
 def analysis_kernel(
     order_ref, levels_ref, stape_ref, otape_ref, mine_ref, one_ref, two_ref, x_ref, mean_ref, obs_ref,
     xo_ref, meano_ref, obso_ref, depo_ref,
-    y_ref, d_ref, r_ref, c_ref, s_ref, u_ref, w_ref, a_ref, p_ref, v_ref, g_ref, dm_ref, do_ref,
+    y_ref, d_ref, r_ref, c_ref, s_ref, u_ref, w_ref, a_ref, p_ref, v_ref, g_ref, dm_ref, do_ref, e_ref, x8_ref, low_ref, mid_ref, qr_ref,
 ):
     eye = iota((B, B), 0) == iota((B, B), 1)
-    low_mask = iota((B, B), 0) >= iota((B, B), 1)
     piece_eye = iota((PIECE, B), 0) == iota((PIECE, B), 1)
     var_eye = iota((PIECE, B), 0) + PIECE == iota((PIECE, B), 1)
     pairs = NB * NBLK * NBLK
@@ -112,7 +144,9 @@
         for k in range(NB):
             line = one_ref[s, 32 + k : 33 + k, :B]
             d_ref[k, pl.ds(at, PIECE), :] = column(line, piece_eye)
-            r_ref[k, pl.ds(at, PIECE), :] = column(line, var_eye)
+            var = column(line, var_eye)
+            r_ref[k, pl.ds(at, PIECE), :] = var
+            e_ref[k, pl.ds(at, PIECE), :] = jnp.sqrt(var)
         return carry
 
     lax.fori_loop(0, ZS * CS, unpack, 0)
@@ -134,7 +168,14 @@
             at = pl.multiple_of(b * B, B)
             a_ref[:, :B] = s_ref[pl.ds(at, B), pl.ds(at, B)]
             a_ref[:, B:] = jnp.where(eye, 1.0, 0.0)
-            factor_block(a_ref, p_ref, w_ref.at[b])
+            last = jnp.maximum(b - 1, 0)
+            seen = pl.multiple_of(last * B, B)
+            steps = doubling_steps(
+                lambda: u_ref[pl.ds(seen, B), pl.ds(seen, B)], low_ref, x8_ref.at[last], mid_ref
+            )
+            hooks = {g + 1: step for g, step in enumerate(steps)}
+            factor_block(a_ref, p_ref, w_ref.at[b], e_ref.at[k, pl.ds(at, B)], x8_ref.at[BASE], hooks)
+            x8_ref[b] = x8_ref[BASE]
             inv = w_ref[b]
             row = mm(inv, s_ref[pl.ds(at, B), :])
             u_ref[pl.ds(at, B), :] = row
@@ -148,19 +189,18 @@
 
         lax.fori_loop(0, NBLK, block_step, 0)
 
-        shifted = []
-        for b in range(NBLK):
-            sl = slice(b * B, b * B + B)
-            low = jnp.where(low_mask, jnp.transpose(u_ref[sl, sl]), 0.0)
-            shifted.append(low + jnp.where(eye, jnp.sqrt(r_ref[k, sl, :]), 0.0))
-        tinv = lower_inverses(shifted)
+        tail = (NBLK - 1) * B
+        for step in doubling_steps(
+            lambda: u_ref[tail : tail + B, tail : tail + B], low_ref, x8_ref.at[NBLK - 1], mid_ref
+        ):
+            step()
 
         v_ref[:, :M] = y_ref[k]
         v_ref[:, M:] = u_ref[:, N:]
         for b in range(NBLK):
             sl = slice(b * B, b * B + B)
             hi = (b + 1) * B
-            v_ref[sl, :M] = mm(tinv[b], v_ref[sl, :M])
+            v_ref[sl, :M] = mm(x8_ref[b], v_ref[sl, :M])
             if b < NBLK - 1:
                 v_ref[hi:, :M] = v_ref[hi:, :M] - mm(u_ref[sl, hi:N], v_ref[sl, :M], 0, 0)
         for b in range(NBLK - 1, -1, -1):
@@ -172,13 +212,18 @@
             v_ref[sl, :] = mm(w_ref[b], rhs, 0, 0)
         for b in range(NBLK):
             sl = slice(b * B, b * B + B)
-            g_ref[b] = mm(y_ref[k, sl, :], v_ref[sl, :], 0, 0) * (1.0 / (M - 1))
-
-        def gain(weight):
-            total = weight(0) * g_ref[0]
+            g_ref[b] = mm3(y_ref[k, sl, :], v_ref[sl, :M], 0, 0) * (1.0 / (M - 1))
+            line = jnp.sum(y_ref[k, sl, :] * wide(v_ref[sl, M:]), axis=0, keepdims=True)
+            qr_ref[b : b + 1, :] = line * (1.0 / (M - 1))
+
+        def update(rows, weight):
+            mat = weight(0) * g_ref[0]
+            line = weight(0) * qr_ref[0:1, :]
             for j in range(1, NBLK):
-                total = total + weight(j) * g_ref[j]
-            return total
+                mat = mat + weight(j) * g_ref[j]
+                line = line + weight(j) * qr_ref[j : j + 1, :]
+            move = jnp.sum(rows * line, axis=1, keepdims=True)
+            return mm3(rows, mat), jnp.broadcast_to(move, (rows.shape[0], B))
 
         def cross_step(n, carry):
             later, i = n // NBLK, n % NBLK
@@ -186,11 +231,12 @@
 
             def weight(j):
                 line = c_ref[pl.ds(later * pairs + k * (NBLK * NBLK) + i * NBLK + j, 1), :]
-                return jnp.concatenate([line] * (WIDE // B), axis=1)
-
-            delta = mm(y_ref[later, pl.ds(at, B), :], gain(weight))
-            y_ref[later, pl.ds(at, B), :] = y_ref[later, pl.ds(at, B), :] - delta[:, :M]
-            d_ref[later, pl.ds(at, B), :] = d_ref[later, pl.ds(at, B), :] - delta[:, M:]
+                return jnp.concatenate([line] * (M // B), axis=1)
+
+            rows = y_ref[later, pl.ds(at, B), :]
+            delta, move = update(rows, weight)
+            y_ref[later, pl.ds(at, B), :] = rows - delta
+            d_ref[later, pl.ds(at, B), :] = d_ref[later, pl.ds(at, B), :] - move
             return carry
 
         lax.fori_loop((k + 1) * NBLK, NB * NBLK, cross_step, 0)
@@ -199,18 +245,18 @@
         def state_step(i, carry):
             at = pl.multiple_of(i * B, B)
             rows = xo_ref[pl.ds(at, B), :]
-            delta = mm(rows, gain(lambda j: levels_ref[stape_ref[i, first + j]]))
-            xo_ref[pl.ds(at, B), :] = rows - delta[:, :M]
-            dm_ref[pl.ds(at, B), :] = dm_ref[pl.ds(at, B), :] + delta[:, M:]
+            delta, move = update(rows, lambda j: levels_ref[stape_ref[i, first + j]])
+            xo_ref[pl.ds(at, B), :] = rows - delta
+            dm_ref[pl.ds(at, B), :] = dm_ref[pl.ds(at, B), :] + move
             return carry
 
         lax.fori_loop(0, x_ref.shape[0] // B, state_step, 0)
         for q in range(KB):
             sl = slice(q * PIECE, q * PIECE + PIECE)
             rows = obso_ref[sl, :]
-            delta = mm(rows, gain(lambda j: levels_ref[otape_ref[q * NBLK + mine_ref[0], first + j]]))
-            obso_ref[sl, :] = rows - delta[:, :M]
-            do_ref[sl, :] = do_ref[sl, :] + delta[:, M:]
+            delta, move = update(rows, lambda j: levels_ref[otape_ref[q * NBLK + mine_ref[0], first + j]])
+            obso_ref[sl, :] = rows - delta
+            do_ref[sl, :] = do_ref[sl, :] + move
         return outer
 
     lax.fori_loop(0, NB, batch_step, 0)
@@ -246,9 +292,14 @@
             scratch(B, 2 * B),
             scratch(B, 2 * B),
             scratch(N, WIDE),
-            scratch(NBLK, M, WIDE),
+            scratch(NBLK, M, M),
             scratch(rows, B),
             scratch(KB * PIECE, B),
+            scratch(NB, N, B),
+            scratch(NBLK + 1, B, B),
+            scratch(B, B),
+            scratch(B, B),
+            scratch(8, M),
         ],
         name="analysis",
     )(order, levels, stape, otape, mine, one, two, x, mean, obs)
@@ -298,11 +349,16 @@
     second = (row == 33) | ((row >= 48) & (row < 80))
     third = (row == 34) | ((row >= 40) & (row < 48)) | (row >= 80)
     far = jnp.where(second, away[1], jnp.where(third, away[2], away[0]))
-    step = size // 2
-    while step:
-        moved = lax.ppermute(block, axis, [(i, (i + step) % size) for i in range(size)])
-        block = jnp.where(far % (2 * step) == 0, block, moved)
-        step //= 2
+    step = size
+    while step > 1:
+        fan = 2 if step == 8 else 4
+        step //= fan
+        moved = {
+            n: lax.ppermute(block, axis, [(i, (i + n * step) % size) for i in range(size)]) for n in range(1, fan)
+        }
+        part = far % (fan * step)
+        for n in moved:
+            block = jnp.where(part // step == n, moved[n], block)
     return block
 
 

time: 214 us -> 205 us (0.958)
  Pallas kernels: 119 us -> 105 us
  starting transfers between devices: 24.6 us -> 32.9 us
  waiting for transfers between devices: 10.6 us -> 7.41 us
    pallas_call x1, Pallas kernels: 117 us -> 103 us  [analysis(): pl.pallas_call(analysis_kernel, out_shape=[shape(rows, M), shape(rows //...]
    ppermute x5 -> x7, starting transfers between devices: 24.6 us -> 32.9 us  [spread(): lax.ppermute(block, axis, [(i, (i + n * step) % size) for i in range(size)])]
    ppermute x5 -> x7, waiting for transfers between devices: 10.6 us -> 7.41 us  [spread(): lax.ppermute(block, axis, [(i, (i + n * step) % size) for i in range(size)])]
  transfers between devices with their start and end apart: 5 -> 7, of which waited for: 4 -> 2; matrix products, arithmetic and copies ran while one was open for 1% -> 1% of each run, Pallas kernels for 0% -> 0%
where the time goes in v1:
time: 205 us; the launch traced here: 204 us
  Pallas kernels  105 us (51%)
  blocking collectives  50.7 us (25%)
  starting transfers between devices  32.9 us (16%)
  waiting for transfers between devices  7.41 us (4%)
  between operations  4.87 us (2%)
    pallas_call x1, Pallas kernels, analysis(): pl.pallas_call(analysis_kernel, out_shape=[shape(rows, M), shape(rows //...  103 us
    ppermute x7, starting transfers between devices, spread(): lax.ppermute(block, axis, [(i, (i + n * step) % size) for i in range(size)])  32.9 us
    all_gather x1, blocking collectives, per_device(): one = lax.all_gather(payload[:48], ('z', 'c'))  32.2 us
    all_gather x1, blocking collectives, per_device(): two = lax.all_gather(payload[48:], ('z', 'c'))  18.5 us
    ppermute x7, waiting for transfers between devices, spread(): lax.ppermute(block, axis, [(i, (i + n * step) % size) for i in range(size)])  7.41 us
  transfers between devices with their start and end apart: 7, of which 2 were waited for; matrix products, arithmetic and copies ran while one was open for 1% of the time, Pallas kernels for 0%

profile of v1, /device:TPU:1, one launch (start us, length us, event | category | flops | bytes accessed | tf_op | source)
XLA Modules:
  0.0 204.3 jit_solution(2964700188524253957)
XLA Ops:
  0.6 0.0 copy-start.2
  0.6 2.1 %prepare.1 = f32[104,256]{1,0:T(8,128)} custom-call(s32[3]{0:T(128)} %order_ref.3, f32[8]{0:T(128)} %levels_ref.3, s32[8,256]{1,0:T(8,128)} %otape_ref.3, f32[2,32,256]{2,1,0:T(8,128)} %obs_ref.1, f32[2,32]{1,0:T(2,128)} %dep_ref.1, f32[2,32]{1,0:T(2,128)} %var_ref.1), custom_call_target="tpu_custom_call" | custom-call | tf_op jit(solution)/shard_map/prepare/pallas_call | solution.py:336
  2.7 0.0 copy-start
  2.7 4.1 %collective-permute-start.2 = (f32[104,256]{1,0:T(8,128)}, f32[104,256]{1,0:T(8,128)S(1)}, u32[]{:S(2)}, u32[]{:S(2)}) collective-permute-start(f32[104,256]{1,0:T(8,128)} %prepare.1), channel_id=1, source_target_pairs={{0,128},{128,256},{256,384},{384,0},{1,129},{129,257},{257,385},{3... | collective-permute-start | bytes 319496 | tf_op jit(solution)/shard_map/ppermute | solution.py:357
  6.8 4.4 %collective-permute-start.1 = (f32[104,256]{1,0:T(8,128)}, f32[104,256]{1,0:T(8,128)S(1)}, u32[]{:S(2)}, u32[]{:S(2)}) collective-permute-start(f32[104,256]{1,0:T(8,128)} %prepare.1), channel_id=1, source_target_pairs={{0,256},{128,384},{256,0},{384,128},{1,257},{129,385},{257,1},{385... | collective-permute-start | bytes 319496 | tf_op jit(solution)/shard_map/ppermute | solution.py:357
  11.1 3.1 %collective-permute-start = (f32[104,256]{1,0:T(8,128)}, f32[104,256]{1,0:T(8,128)S(1)}, u32[]{:S(2)}, u32[]{:S(2)}) collective-permute-start(f32[104,256]{1,0:T(8,128)} %prepare.1), channel_id=1, source_target_pairs={{0,384},{128,0},{256,128},{384,256},{1,385},{129,1},{257,129},{385... | collective-permute-start | bytes 319496 | tf_op jit(solution)/shard_map/ppermute | solution.py:357
  14.2 0.0 copy-done.2
  14.3 0.6 fusion.8
  16.9 0.6 fusion.7
  19.5 0.0 collective-permute-done.2
  19.5 0.0 collective-permute-done.1
  19.5 0.0 collective-permute-done
  19.5 0.0 copy-done
  19.5 0.1 select_select_fusion.3
  19.6 7.5 %collective-permute-start.3 = (f32[104,256]{1,0:T(8,128)S(1)}, f32[104,256]{1,0:T(8,128)S(1)}, u32[]{:S(2)}, u32[]{:S(2)}) collective-permute-start(f32[104,256]{1,0:T(8,128)S(1)} %select_select_fusion.3), channel_id=1, source_target_pairs={{0,64},{16,80},{32,96},{48,112},{64,0},{80,16},{96,32},{112,48},{1... | collective-permute-start | bytes 319496 | tf_op jit(solution)/shard_map/ppermute | solution.py:357
  27.1 2.2 %collective-permute-done.3 = f32[104,256]{1,0:T(8,128)S(1)} collective-permute-done((f32[104,256]{1,0:T(8,128)S(1)}, f32[104,256]{1,0:T(8,128)S(1)}, u32[]{:S(2)}, u32[]{:S(2)}) %collective-permute-start.3) | collective-permute-done | bytes 106528 | tf_op jit(solution)/shard_map/ppermute | solution.py:357
  29.3 0.1 fusion.6
  29.4 3.0 %collective-permute-start.6 = (f32[104,256]{1,0:T(8,128)S(1)}, f32[104,256]{1,0:T(8,128)S(1)}, u32[]{:S(2)}, u32[]{:S(2)}) collective-permute-start(f32[104,256]{1,0:T(8,128)S(1)} %fusion.6), channel_id=1, source_target_pairs={{0,16},{16,32},{32,48},{48,64},{64,80},{80,96},{96,112},{112,0},{1... | collective-permute-start | bytes 319496 | tf_op jit(solution)/shard_map/ppermute | solution.py:357
  32.5 4.5 %collective-permute-start.5 = (f32[104,256]{1,0:T(8,128)S(1)}, f32[104,256]{1,0:T(8,128)S(1)}, u32[]{:S(2)}, u32[]{:S(2)}) collective-permute-start(f32[104,256]{1,0:T(8,128)S(1)} %fusion.6), channel_id=1, source_target_pairs={{0,32},{16,48},{32,64},{48,80},{64,96},{80,112},{96,0},{112,16},{1... | collective-permute-start | bytes 319496 | tf_op jit(solution)/shard_map/ppermute | solution.py:357
  37.0 6.5 %collective-permute-start.4 = (f32[104,256]{1,0:T(8,128)S(1)}, f32[104,256]{1,0:T(8,128)S(1)}, u32[]{:S(2)}, u32[]{:S(2)}) collective-permute-start(f32[104,256]{1,0:T(8,128)S(1)} %fusion.6), channel_id=1, source_target_pairs={{0,48},{16,64},{32,80},{48,96},{64,112},{80,0},{96,16},{112,32},{1... | collective-permute-start | bytes 319496 | tf_op jit(solution)/shard_map/ppermute | solution.py:357
  43.5 0.0 collective-permute-done.6
  43.5 0.0 collective-permute-done.5
  43.5 5.2 %collective-permute-done.4 = f32[104,256]{1,0:T(8,128)S(1)} collective-permute-done((f32[104,256]{1,0:T(8,128)S(1)}, f32[104,256]{1,0:T(8,128)S(1)}, u32[]{:S(2)}, u32[]{:S(2)}) %collective-permute-start.4) | collective-permute-done | bytes 106528 | tf_op jit(solution)/shard_map/ppermute | solution.py:357
  48.7 0.1 select_select_fusion.2
  48.9 32.2 %all-gather = f32[768,256]{1,0:T(8,128)} all-gather(f32[48,256]{1,0:T(8,128)S(1)} %slice.36), channel_id=2, replica_groups=mesh['x'=4,'y'=8,'z'=8,'c'=2] {'z','c'}, dimensions={0}, use_global_device_ids=true | all-gather | bytes 835584 | tf_op jit(solution)/shard_map/all_gather | solution.py:371
  81.1 18.5 %all-gather.1 = f32[896,256]{1,0:T(8,128)} all-gather(f32[56,256]{1,0:T(8,128)S(1)} %slice.37), channel_id=3, replica_groups=mesh['x'=4,'y'=8,'z'=8,'c'=2] {'z','c'}, dimensions={0}, use_global_device_ids=true | all-gather | bytes 974848 | tf_op jit(solution)/shard_map/all_gather | solution.py:372
  99.5 102.8 %analysis.1 = (f32[1024,256]{1,0:T(8,128)}, f32[8,128]{1,0:T(8,128)}, f32[64,256]{1,0:T(8,128)}, f32[2,128]{1,0:T(2,128)}) custom-call(s32[3]{0:T(128)} %order_ref.3, f32[8]{0:T(128)} %levels_ref.3, s32[8,256]{1,0:T(8,128)} %stape_ref.1, s32[8,256]{1,0:T(8,128)} %otape_ref.3, s32[1]{0:T(128)} %bitcast.mine_ref, f32[16,48,256]{2,1,0:T(8,128)} %bitcast.14, ...), custom_call_target="tpu_custom_call" | custom-call | tf_op jit(solution)/shard_map/analysis/pallas_call | solution.py:279
  202.4 0.0 copy-start.1
  202.4 0.7 copy-done.1
  203.0 1.2 slice_subtract_fusion
  (7 shorter events, 0.1 us)
Async XLA Ops:
  0.6 13.6 %copy-start.2 = (s32[3]{0:T(128)S(1)}, s32[3]{0:T(128)}, u32[]{:S(2)}) copy-start(s32[3]{0:T(128)} %order_ref.3) | copy-start | bytes 40
  2.7 16.8 %copy-start = (f32[104,256]{1,0:T(8,128)S(1)}, f32[104,256]{1,0:T(8,128)}, u32[]{:S(2)}) copy-start(f32[104,256]{1,0:T(8,128)} %prepare.1) | copy-start | bytes 319492
  2.7 16.8 %collective-permute-start.2 = (f32[104,256]{1,0:T(8,128)}, f32[104,256]{1,0:T(8,128)S(1)}, u32[]{:S(2)}, u32[]{:S(2)}) collective-permute-start(f32[104,256]{1,0:T(8,128)} %prepare.1), channel_id=1, source_target_pairs={{0,128},{128,256},{256,384},{384,0},{1,129},{129,257},{257,385},{3... | collective-permute-start | bytes 319496 | tf_op jit(solution)/shard_map/ppermute | solution.py:357
  6.8 12.7 %collective-permute-start.1 = (f32[104,256]{1,0:T(8,128)}, f32[104,256]{1,0:T(8,128)S(1)}, u32[]{:S(2)}, u32[]{:S(2)}) collective-permute-start(f32[104,256]{1,0:T(8,128)} %prepare.1), channel_id=1, source_target_pairs={{0,256},{128,384},{256,0},{384,128},{1,257},{129,385},{257,1},{385... | collective-permute-start | bytes 319496 | tf_op jit(solution)/shard_map/ppermute | solution.py:357
  11.1 8.4 %collective-permute-start = (f32[104,256]{1,0:T(8,128)}, f32[104,256]{1,0:T(8,128)S(1)}, u32[]{:S(2)}, u32[]{:S(2)}) collective-permute-start(f32[104,256]{1,0:T(8,128)} %prepare.1), channel_id=1, source_target_pairs={{0,384},{128,0},{256,128},{384,256},{1,385},{129,1},{257,129},{385... | collective-permute-start | bytes 319496 | tf_op jit(solution)/shard_map/ppermute | solution.py:357
  19.6 9.6 %collective-permute-start.3 = (f32[104,256]{1,0:T(8,128)S(1)}, f32[104,256]{1,0:T(8,128)S(1)}, u32[]{:S(2)}, u32[]{:S(2)}) collective-permute-start(f32[104,256]{1,0:T(8,128)S(1)} %select_select_fusion.3), channel_id=1, source_target_pairs={{0,64},{16,80},{32,96},{48,112},{64,0},{80,16},{96,32},{112,48},{1... | collective-permute-start | bytes 319496 | tf_op jit(solution)/shard_map/ppermute | solution.py:357
  29.4 14.0 %collective-permute-start.6 = (f32[104,256]{1,0:T(8,128)S(1)}, f32[104,256]{1,0:T(8,128)S(1)}, u32[]{:S(2)}, u32[]{:S(2)}) collective-permute-start(f32[104,256]{1,0:T(8,128)S(1)} %fusion.6), channel_id=1, source_target_pairs={{0,16},{16,32},{32,48},{48,64},{64,80},{80,96},{96,112},{112,0},{1... | collective-permute-start | bytes 319496 | tf_op jit(solution)/shard_map/ppermute | solution.py:357
  32.5 11.0 %collective-permute-start.5 = (f32[104,256]{1,0:T(8,128)S(1)}, f32[104,256]{1,0:T(8,128)S(1)}, u32[]{:S(2)}, u32[]{:S(2)}) collective-permute-start(f32[104,256]{1,0:T(8,128)S(1)} %fusion.6), channel_id=1, source_target_pairs={{0,32},{16,48},{32,64},{48,80},{64,96},{80,112},{96,0},{112,16},{1... | collective-permute-start | bytes 319496 | tf_op jit(solution)/shard_map/ppermute | solution.py:357
  37.0 11.8 %collective-permute-start.4 = (f32[104,256]{1,0:T(8,128)S(1)}, f32[104,256]{1,0:T(8,128)S(1)}, u32[]{:S(2)}, u32[]{:S(2)}) collective-permute-start(f32[104,256]{1,0:T(8,128)S(1)} %fusion.6), channel_id=1, source_target_pairs={{0,48},{16,64},{32,80},{48,96},{64,112},{80,0},{96,16},{112,32},{1... | collective-permute-start | bytes 319496 | tf_op jit(solution)/shard_map/ppermute | solution.py:357
  202.4 0.7 copy-start.1

commit v2 on v1

--- a/solution.py
+++ b/solution.py
@@ -48,18 +48,21 @@
     return hi, mid, (rest - mid.astype(F32)).astype(jnp.bfloat16)
 
 
-def factor_block(a_ref, p_ref, w_ref, root_ref, base_ref, hooks):
+def factor_block(a_ref, p_ref, w_ref, root_ref, base_ref, n_ref, c_ref, hooks):
     groups = B // 8
     lane = iota((8, B), 1)
     rows = [jnp.broadcast_to(a_ref[s : s + 1, :], (8, 2 * B)) for s in range(8)]
+    corner = a_ref[0:8, :B]
     for g in range(groups):
         j0 = 8 * g
+        slot = 64 * (g % 2)
+        for t in range(8):
+            c_ref[slot + 8 * t : slot + 8 * t + 8, :] = jnp.broadcast_to(corner[:, j0 + t : j0 + t + 1], (8, B))
         d = {}
         for s in range(8):
             for t in range(s + 1):
-                d[s, t] = jnp.broadcast_to(rows[t][:, j0 + s : j0 + s + 1], (8, B))
-        if g < groups - 1:
-            ahead = [jnp.broadcast_to(a_ref[j0 + 8 + s : j0 + 9 + s, :], (8, 2 * B)) for s in range(8)]
+                at = slot + 8 * t + s
+                d[s, t] = jnp.broadcast_to(c_ref[at : at + 1, :], (8, B))
         low, diag = {}, []
         for t in range(8):
             inv = lax.rsqrt(d[t, t])
@@ -75,8 +78,18 @@
             w_ref[j0 + t : j0 + t + 1, :] = done[:1, B:]
             if g < groups - 1:
                 p_ref[j0 + t : j0 + t + 1, :] = done[:1, :]
-                for s in range(8):
-                    ahead[s] = ahead[s] - wide(jnp.broadcast_to(done[:, j0 + 8 + s : j0 + 9 + s], (8, B))) * done
+        if g < groups - 1:
+            panel = p_ref[j0 : j0 + 8, :]
+            ahead = []
+            turn = 8 * (g % 2)
+            for s in range(8):
+                j1 = j0 + 8 + s
+                fix = wide(jnp.broadcast_to(panel[:, j1 : j1 + 1], (8, B))) * panel
+                for step in (4, 2, 1):
+                    fix = fix + pltpu.roll(fix, step, 0)
+                ahead.append(jnp.broadcast_to(a_ref[j1 : j1 + 1, :], (8, 2 * B)) - fix)
+                n_ref[turn + s : turn + s + 1, :] = ahead[s][:1, :B]
+            corner = n_ref[turn : turn + 8, :]
         small = []
         for s in range(8):
             row = jnp.where(lane == j0 + s, 1.0, 0.0)
@@ -117,13 +130,24 @@
     return steps
 
 
+def forward_steps(cols, y, v_ref, out_ref, x_ref, part_ref, first_row):
+    def above():
+        factor = jnp.where(iota((N, B), 0) < first_row, cols(), 0.0)
+        part_ref[...] = y() - mm(factor, v_ref[:, :M], 0, 0)
+
+    def solve():
+        out_ref[...] = mm(x_ref[...], part_ref[...])
+
+    return [above, solve]
+
+
 BASE = NBLK
 
 
 def analysis_kernel(
     order_ref, levels_ref, stape_ref, otape_ref, mine_ref, one_ref, two_ref, x_ref, mean_ref, obs_ref,
     xo_ref, meano_ref, obso_ref, depo_ref,
-    y_ref, d_ref, r_ref, c_ref, s_ref, u_ref, w_ref, a_ref, p_ref, v_ref, g_ref, dm_ref, do_ref, e_ref, x8_ref, low_ref, mid_ref, qr_ref,
+    y_ref, d_ref, r_ref, c_ref, s_ref, u_ref, w_ref, a_ref, p_ref, v_ref, g_ref, dm_ref, do_ref, e_ref, x8_ref, low_ref, mid_ref, qr_ref, n_ref, k_ref, q_ref, part_ref, z_ref,
 ):
     eye = iota((B, B), 0) == iota((B, B), 1)
     piece_eye = iota((PIECE, B), 0) == iota((PIECE, B), 1)
@@ -156,8 +180,40 @@
     obso_ref[...] = obs_ref[...]
     dm_ref[...] = jnp.zeros_like(dm_ref)
     do_ref[...] = jnp.zeros_like(do_ref)
+    for ref in (u_ref, x8_ref, v_ref, g_ref, qr_ref):
+        ref[...] = jnp.zeros_like(ref)
+
+    def update(rows, slot, weight):
+        mat = weight(0) * g_ref[slot, 0]
+        line = weight(0) * qr_ref[slot, 0:1, :]
+        for j in range(1, NBLK):
+            mat = mat + weight(j) * g_ref[slot, j]
+            line = line + weight(j) * qr_ref[slot, j : j + 1, :]
+        move = jnp.sum(rows * line, axis=1, keepdims=True)
+        return mm3(rows, mat), jnp.broadcast_to(move, (rows.shape[0], B))
+
+    def own_steps(k, slot):
+        first = order_ref[k] * NBLK
+
+        def state(i):
+            sl = slice(i * B, i * B + B)
+            rows = xo_ref[sl, :]
+            delta, move = update(rows, slot, lambda j: levels_ref[stape_ref[i, first + j]])
+            xo_ref[sl, :] = rows - delta
+            dm_ref[sl, :] = dm_ref[sl, :] + move
+
+        def observed(q):
+            sl = slice(q * PIECE, q * PIECE + PIECE)
+            rows = obso_ref[sl, :]
+            delta, move = update(rows, slot, lambda j: levels_ref[otape_ref[q * NBLK + mine_ref[0], first + j]])
+            obso_ref[sl, :] = rows - delta
+            do_ref[sl, :] = do_ref[sl, :] + move
+
+        steps = [lambda i=i: state(i) for i in range(x_ref.shape[0] // B)]
+        return steps + [lambda q=q: observed(q) for q in range(KB)]
 
     def batch_step(k, outer):
+        slot = k % 2
         s_ref[:, :N] = mm(y_ref[k], y_ref[k], 1, 1) * (1.0 / (M - 1))
         s_ref[:, N:] = d_ref[k]
         for b in range(NBLK):
@@ -173,8 +229,12 @@
             steps = doubling_steps(
                 lambda: u_ref[pl.ds(seen, B), pl.ds(seen, B)], low_ref, x8_ref.at[last], mid_ref
             )
+            steps += forward_steps(
+                lambda: u_ref[:, pl.ds(seen, B)], lambda: y_ref[k, pl.ds(seen, B), :],
+                v_ref, v_ref.at[pl.ds(seen, B)], x8_ref.at[last], part_ref, seen,
+            )
             hooks = {g + 1: step for g, step in enumerate(steps)}
-            factor_block(a_ref, p_ref, w_ref.at[b], e_ref.at[k, pl.ds(at, B)], x8_ref.at[BASE], hooks)
+            factor_block(a_ref, p_ref, w_ref.at[b], e_ref.at[k, pl.ds(at, B)], x8_ref.at[BASE], n_ref, k_ref, hooks)
             x8_ref[b] = x8_ref[BASE]
             inv = w_ref[b]
             row = mm(inv, s_ref[pl.ds(at, B), :])
@@ -184,46 +244,43 @@
                 def _():
                     lo = (c + 1) * B
                     q = mm(inv, u_ref[lo - B : lo, lo:], 0, 0)
+                    q_ref[lo - B : lo, lo:] = q
                     s_ref[lo:, lo:] = s_ref[lo:, lo:] - mm(s_ref[lo:, lo - B : lo], q)
             return carry
 
         lax.fori_loop(0, NBLK, block_step, 0)
 
         tail = (NBLK - 1) * B
-        for step in doubling_steps(
+        solving = doubling_steps(
             lambda: u_ref[tail : tail + B, tail : tail + B], low_ref, x8_ref.at[NBLK - 1], mid_ref
-        ):
-            step()
-
-        v_ref[:, :M] = y_ref[k]
-        v_ref[:, M:] = u_ref[:, N:]
+        )
+        above, solve = forward_steps(
+            lambda: u_ref[:, tail:N], lambda: y_ref[k, tail:N, :],
+            v_ref, v_ref.at[tail:N], x8_ref.at[NBLK - 1], part_ref, tail,
+        )
+        owed = own_steps(jnp.maximum(k - 1, 0), 1 - slot)
+        above()
+        while solving or owed:
+            if solving:
+                solving.pop(0)()
+            if owed:
+                owed.pop(0)()
+        for b in range(NBLK - 1):
+            sl = slice(b * B, b * B + B)
+            z_ref[sl, :M] = mm(w_ref[b], v_ref[sl, :], 0, 0)
+            z_ref[sl, M:] = q_ref[sl, N:]
+        solve()
+        z_ref[tail:N, :M] = mm(w_ref[NBLK - 1], v_ref[tail:N, :], 0, 0)
+        z_ref[tail:N, M:] = mm(w_ref[NBLK - 1], u_ref[tail:N, N:], 0, 0)
+        for b in range(NBLK - 2, -1, -1):
+            sl = slice(b * B, b * B + B)
+            hi = (b + 1) * B
+            z_ref[sl, :] = z_ref[sl, :] - mm(q_ref[sl, hi:N], z_ref[hi:N, :])
         for b in range(NBLK):
             sl = slice(b * B, b * B + B)
-            hi = (b + 1) * B
-            v_ref[sl, :M] = mm(x8_ref[b], v_ref[sl, :M])
-            if b < NBLK - 1:
-                v_ref[hi:, :M] = v_ref[hi:, :M] - mm(u_ref[sl, hi:N], v_ref[sl, :M], 0, 0)
-        for b in range(NBLK - 1, -1, -1):
-            sl = slice(b * B, b * B + B)
-            hi = (b + 1) * B
-            rhs = v_ref[sl, :]
-            if b < NBLK - 1:
-                rhs = rhs - mm(u_ref[sl, hi:N], v_ref[hi:, :])
-            v_ref[sl, :] = mm(w_ref[b], rhs, 0, 0)
-        for b in range(NBLK):
-            sl = slice(b * B, b * B + B)
-            g_ref[b] = mm3(y_ref[k, sl, :], v_ref[sl, :M], 0, 0) * (1.0 / (M - 1))
-            line = jnp.sum(y_ref[k, sl, :] * wide(v_ref[sl, M:]), axis=0, keepdims=True)
-            qr_ref[b : b + 1, :] = line * (1.0 / (M - 1))
-
-        def update(rows, weight):
-            mat = weight(0) * g_ref[0]
-            line = weight(0) * qr_ref[0:1, :]
-            for j in range(1, NBLK):
-                mat = mat + weight(j) * g_ref[j]
-                line = line + weight(j) * qr_ref[j : j + 1, :]
-            move = jnp.sum(rows * line, axis=1, keepdims=True)
-            return mm3(rows, mat), jnp.broadcast_to(move, (rows.shape[0], B))
+            g_ref[slot, b] = mm3(y_ref[k, sl, :], z_ref[sl, :M], 0, 0) * (1.0 / (M - 1))
+            line = jnp.sum(y_ref[k, sl, :] * wide(z_ref[sl, M:]), axis=0, keepdims=True)
+            qr_ref[slot, b : b + 1, :] = line * (1.0 / (M - 1))
 
         def cross_step(n, carry):
             later, i = n // NBLK, n % NBLK
@@ -234,32 +291,17 @@
                 return jnp.concatenate([line] * (M // B), axis=1)
 
             rows = y_ref[later, pl.ds(at, B), :]
-            delta, move = update(rows, weight)
+            delta, move = update(rows, slot, weight)
             y_ref[later, pl.ds(at, B), :] = rows - delta
             d_ref[later, pl.ds(at, B), :] = d_ref[later, pl.ds(at, B), :] - move
             return carry
 
         lax.fori_loop((k + 1) * NBLK, NB * NBLK, cross_step, 0)
-        first = order_ref[k] * NBLK
-
-        def state_step(i, carry):
-            at = pl.multiple_of(i * B, B)
-            rows = xo_ref[pl.ds(at, B), :]
-            delta, move = update(rows, lambda j: levels_ref[stape_ref[i, first + j]])
-            xo_ref[pl.ds(at, B), :] = rows - delta
-            dm_ref[pl.ds(at, B), :] = dm_ref[pl.ds(at, B), :] + move
-            return carry
-
-        lax.fori_loop(0, x_ref.shape[0] // B, state_step, 0)
-        for q in range(KB):
-            sl = slice(q * PIECE, q * PIECE + PIECE)
-            rows = obso_ref[sl, :]
-            delta, move = update(rows, lambda j: levels_ref[otape_ref[q * NBLK + mine_ref[0], first + j]])
-            obso_ref[sl, :] = rows - delta
-            do_ref[sl, :] = do_ref[sl, :] + move
         return outer
 
     lax.fori_loop(0, NB, batch_step, 0)
+    for step in own_steps(NB - 1, (NB - 1) % 2):
+        step()
 
     for i in range(x_ref.shape[0] // B):
         sl = slice(i * B, i * B + B)
@@ -291,15 +333,20 @@
             scratch(NBLK, B, B),
             scratch(B, 2 * B),
             scratch(B, 2 * B),
-            scratch(N, WIDE),
-            scratch(NBLK, M, M),
+            scratch(N, M),
+            scratch(2, NBLK, M, M),
             scratch(rows, B),
             scratch(KB * PIECE, B),
             scratch(NB, N, B),
             scratch(NBLK + 1, B, B),
             scratch(B, B),
             scratch(B, B),
-            scratch(8, M),
+            scratch(2, 8, M),
+            scratch(16, B),
+            scratch(2 * 64, B),
+            scratch(N, N + B),
+            scratch(B, M),
+            scratch(N, WIDE),
         ],
         name="analysis",
     )(order, levels, stape, otape, mine, one, two, x, mean, obs)
@@ -349,16 +396,11 @@
     second = (row == 33) | ((row >= 48) & (row < 80))
     third = (row == 34) | ((row >= 40) & (row < 48)) | (row >= 80)
     far = jnp.where(second, away[1], jnp.where(third, away[2], away[0]))
-    step = size
-    while step > 1:
-        fan = 2 if step == 8 else 4
-        step //= fan
-        moved = {
-            n: lax.ppermute(block, axis, [(i, (i + n * step) % size) for i in range(size)]) for n in range(1, fan)
-        }
-        part = far % (fan * step)
-        for n in moved:
-            block = jnp.where(part // step == n, moved[n], block)
+    step = size // 2
+    while step:
+        moved = lax.ppermute(block, axis, [(i, (i + step) % size) for i in range(size)])
+        block = jnp.where(far % (2 * step) == 0, block, moved)
+        step //= 2
     return block
 
 

time: 205 us -> 190 us (0.927)
  Pallas kernels: 105 us -> 94.8 us
  starting transfers between devices: 32.9 us -> 24.6 us
  waiting for transfers between devices: 7.41 us -> 10.6 us
    pallas_call x1, Pallas kernels: 103 us -> 92.8 us  [analysis(): pl.pallas_call(analysis_kernel, out_shape=[shape(rows, M), shape(rows //...]
    ppermute x7 -> x5, starting transfers between devices: 32.9 us -> 24.6 us  [spread(): lax.ppermute(block, axis, [(i, (i + step) % size) for i in range(size)])]
    ppermute x7 -> x5, waiting for transfers between devices: 7.41 us -> 10.6 us  [spread(): lax.ppermute(block, axis, [(i, (i + step) % size) for i in range(size)])]
  transfers between devices with their start and end apart: 7 -> 5, of which waited for: 2 -> 4; matrix products, arithmetic and copies ran while one was open for 1% -> 1% of each run, Pallas kernels for 0% -> 0%
where the time goes in v2:
time: 190 us; the launch traced here: 189 us
  Pallas kernels  94.8 us (50%)
  blocking collectives  50.7 us (27%)
  starting transfers between devices  24.6 us (13%)
  waiting for transfers between devices  10.6 us (6%)
  between operations  4.81 us (3%)
    pallas_call x1, Pallas kernels, analysis(): pl.pallas_call(analysis_kernel, out_shape=[shape(rows, M), shape(rows //...  92.8 us
    all_gather x1, blocking collectives, per_device(): one = lax.all_gather(payload[:48], ('z', 'c'))  32.2 us
    ppermute x5, starting transfers between devices, spread(): lax.ppermute(block, axis, [(i, (i + step) % size) for i in range(size)])  24.6 us
    all_gather x1, blocking collectives, per_device(): two = lax.all_gather(payload[48:], ('z', 'c'))  18.5 us
    ppermute x5, waiting for transfers between devices, spread(): lax.ppermute(block, axis, [(i, (i + step) % size) for i in range(size)])  10.6 us
  transfers between devices with their start and end apart: 5, of which 4 were waited for; matrix products, arithmetic and copies ran while one was open for 1% of the time, Pallas kernels for 0%

profile of v2, /device:TPU:1, one launch (start us, length us, event | category | flops | bytes accessed | tf_op | source)
XLA Modules:
  0.0 189.2 jit_solution(13610488627863296810)
XLA Ops:
  0.6 0.0 copy-start.2
  0.6 2.1 %prepare.1 = f32[104,256]{1,0:T(8,128)} custom-call(s32[3]{0:T(128)} %order_ref.3, f32[8]{0:T(128)} %levels_ref.3, s32[8,256]{1,0:T(8,128)} %otape_ref.3, f32[2,32,256]{2,1,0:T(8,128)} %obs_ref.1, f32[2,32]{1,0:T(2,128)} %dep_ref.1, f32[2,32]{1,0:T(2,128)} %var_ref.1), custom_call_target="tpu_custom_call" | custom-call | tf_op jit(solution)/shard_map/prepare/pallas_call | solution.py:383
  2.7 0.0 copy-start
  2.7 5.6 %collective-permute-start = (f32[104,256]{1,0:T(8,128)}, f32[104,256]{1,0:T(8,128)S(1)}, u32[]{:S(2)}, u32[]{:S(2)}) collective-permute-start(f32[104,256]{1,0:T(8,128)} %prepare.1), channel_id=1, source_target_pairs={{0,256},{128,384},{256,0},{384,128},{1,257},{129,385},{257,1},{385... | collective-permute-start | bytes 319496 | tf_op jit(solution)/shard_map/ppermute | solution.py:401
  8.3 0.0 copy-done.2
  8.4 0.6 fusion.16
  11.0 0.0 collective-permute-done
  11.0 0.0 copy-done
  11.0 0.1 fusion.10
  11.1 3.2 %collective-permute-start.1 = (f32[104,256]{1,0:T(8,128)S(1)}, f32[104,256]{1,0:T(8,128)S(1)}, u32[]{:S(2)}, u32[]{:S(2)}) collective-permute-start(f32[104,256]{1,0:T(8,128)S(1)} %fusion.10), channel_id=1, source_target_pairs={{0,128},{128,256},{256,384},{384,0},{1,129},{129,257},{257,385},{3... | collective-permute-start | bytes 319496 | tf_op jit(solution)/shard_map/ppermute | solution.py:401
  14.3 0.6 fusion.15
  16.9 1.5 collective-permute-done.1
  18.4 0.1 fusion.11
  18.5 6.9 %collective-permute-start.2 = (f32[104,256]{1,0:T(8,128)S(1)}, f32[104,256]{1,0:T(8,128)S(1)}, u32[]{:S(2)}, u32[]{:S(2)}) collective-permute-start(f32[104,256]{1,0:T(8,128)S(1)} %fusion.11), channel_id=1, source_target_pairs={{0,64},{16,80},{32,96},{48,112},{64,0},{80,16},{96,32},{112,48},{1... | collective-permute-start | bytes 319496 | tf_op jit(solution)/shard_map/ppermute | solution.py:401
  25.5 2.5 %collective-permute-done.2 = f32[104,256]{1,0:T(8,128)S(1)} collective-permute-done((f32[104,256]{1,0:T(8,128)S(1)}, f32[104,256]{1,0:T(8,128)S(1)}, u32[]{:S(2)}, u32[]{:S(2)}) %collective-permute-start.2) | collective-permute-done | bytes 106528 | tf_op jit(solution)/shard_map/ppermute | solution.py:401
  28.0 0.1 fusion.12
  28.1 4.7 %collective-permute-start.3 = (f32[104,256]{1,0:T(8,128)S(1)}, f32[104,256]{1,0:T(8,128)S(1)}, u32[]{:S(2)}, u32[]{:S(2)}) collective-permute-start(f32[104,256]{1,0:T(8,128)S(1)} %fusion.12), channel_id=1, source_target_pairs={{0,32},{16,48},{32,64},{48,80},{64,96},{80,112},{96,0},{112,16},{1... | collective-permute-start | bytes 319496 | tf_op jit(solution)/shard_map/ppermute | solution.py:401
  32.8 4.1 %collective-permute-done.3 = f32[104,256]{1,0:T(8,128)S(1)} collective-permute-done((f32[104,256]{1,0:T(8,128)S(1)}, f32[104,256]{1,0:T(8,128)S(1)}, u32[]{:S(2)}, u32[]{:S(2)}) %collective-permute-start.3) | collective-permute-done | bytes 106528 | tf_op jit(solution)/shard_map/ppermute | solution.py:401
  36.9 0.1 fusion.13
  37.0 4.1 %collective-permute-start.4 = (f32[104,256]{1,0:T(8,128)S(1)}, f32[104,256]{1,0:T(8,128)S(1)}, u32[]{:S(2)}, u32[]{:S(2)}) collective-permute-start(f32[104,256]{1,0:T(8,128)S(1)} %fusion.13), channel_id=1, source_target_pairs={{0,16},{16,32},{32,48},{48,64},{64,80},{80,96},{96,112},{112,0},{1... | collective-permute-start | bytes 319496 | tf_op jit(solution)/shard_map/ppermute | solution.py:401
  41.2 2.5 %collective-permute-done.4 = f32[104,256]{1,0:T(8,128)S(1)} collective-permute-done((f32[104,256]{1,0:T(8,128)S(1)}, f32[104,256]{1,0:T(8,128)S(1)}, u32[]{:S(2)}, u32[]{:S(2)}) %collective-permute-start.4) | collective-permute-done | bytes 106528 | tf_op jit(solution)/shard_map/ppermute | solution.py:401
  43.7 0.1 fusion.14
  43.8 32.2 %all-gather = f32[768,256]{1,0:T(8,128)} all-gather(f32[48,256]{1,0:T(8,128)S(1)} %slice.36), channel_id=2, replica_groups=mesh['x'=4,'y'=8,'z'=8,'c'=2] {'z','c'}, dimensions={0}, use_global_device_ids=true | all-gather | bytes 835584 | tf_op jit(solution)/shard_map/all_gather | solution.py:413
  76.1 18.5 %all-gather.1 = f32[896,256]{1,0:T(8,128)} all-gather(f32[56,256]{1,0:T(8,128)S(1)} %slice.37), channel_id=3, replica_groups=mesh['x'=4,'y'=8,'z'=8,'c'=2] {'z','c'}, dimensions={0}, use_global_device_ids=true | all-gather | bytes 974848 | tf_op jit(solution)/shard_map/all_gather | solution.py:414
  94.5 92.8 %analysis.1 = (f32[1024,256]{1,0:T(8,128)}, f32[8,128]{1,0:T(8,128)}, f32[64,256]{1,0:T(8,128)}, f32[2,128]{1,0:T(2,128)}) custom-call(s32[3]{0:T(128)} %order_ref.3, f32[8]{0:T(128)} %levels_ref.3, s32[8,256]{1,0:T(8,128)} %stape_ref.1, s32[8,256]{1,0:T(8,128)} %otape_ref.3, s32[1]{0:T(128)} %bitcast.mine_ref, f32[16,48,256]{2,1,0:T(8,128)} %bitcast.14, ...), custom_call_target="tpu_custom_call" | custom-call | tf_op jit(solution)/shard_map/analysis/pallas_call | solution.py:321
  187.3 0.0 copy-start.1
  187.3 0.7 copy-done.1
  188.0 1.2 slice_subtract_fusion
  (7 shorter events, 0.1 us)
Async XLA Ops:
  0.6 7.7 %copy-start.2 = (s32[3]{0:T(128)S(1)}, s32[3]{0:T(128)}, u32[]{:S(2)}) copy-start(s32[3]{0:T(128)} %order_ref.3) | copy-start | bytes 40
  2.7 8.3 %copy-start = (f32[104,256]{1,0:T(8,128)S(1)}, f32[104,256]{1,0:T(8,128)}, u32[]{:S(2)}) copy-start(f32[104,256]{1,0:T(8,128)} %prepare.1) | copy-start | bytes 319492
  2.7 8.3 %collective-permute-start = (f32[104,256]{1,0:T(8,128)}, f32[104,256]{1,0:T(8,128)S(1)}, u32[]{:S(2)}, u32[]{:S(2)}) collective-permute-start(f32[104,256]{1,0:T(8,128)} %prepare.1), channel_id=1, source_target_pairs={{0,256},{128,384},{256,0},{384,128},{1,257},{129,385},{257,1},{385... | collective-permute-start | bytes 319496 | tf_op jit(solution)/shard_map/ppermute | solution.py:401
  11.1 7.3 %collective-permute-start.1 = (f32[104,256]{1,0:T(8,128)S(1)}, f32[104,256]{1,0:T(8,128)S(1)}, u32[]{:S(2)}, u32[]{:S(2)}) collective-permute-start(f32[104,256]{1,0:T(8,128)S(1)} %fusion.10), channel_id=1, source_target_pairs={{0,128},{128,256},{256,384},{384,0},{1,129},{129,257},{257,385},{3... | collective-permute-start | bytes 319496 | tf_op jit(solution)/shard_map/ppermute | solution.py:401
  18.5 9.5 %collective-permute-start.2 = (f32[104,256]{1,0:T(8,128)S(1)}, f32[104,256]{1,0:T(8,128)S(1)}, u32[]{:S(2)}, u32[]{:S(2)}) collective-permute-start(f32[104,256]{1,0:T(8,128)S(1)} %fusion.11), channel_id=1, source_target_pairs={{0,64},{16,80},{32,96},{48,112},{64,0},{80,16},{96,32},{112,48},{1... | collective-permute-start | bytes 319496 | tf_op jit(solution)/shard_map/ppermute | solution.py:401
  28.1 8.8 %collective-permute-start.3 = (f32[104,256]{1,0:T(8,128)S(1)}, f32[104,256]{1,0:T(8,128)S(1)}, u32[]{:S(2)}, u32[]{:S(2)}) collective-permute-start(f32[104,256]{1,0:T(8,128)S(1)} %fusion.12), channel_id=1, source_target_pairs={{0,32},{16,48},{32,64},{48,80},{64,96},{80,112},{96,0},{112,16},{1... | collective-permute-start | bytes 319496 | tf_op jit(solution)/shard_map/ppermute | solution.py:401
  37.0 6.7 %collective-permute-start.4 = (f32[104,256]{1,0:T(8,128)S(1)}, f32[104,256]{1,0:T(8,128)S(1)}, u32[]{:S(2)}, u32[]{:S(2)}) collective-permute-start(f32[104,256]{1,0:T(8,128)S(1)} %fusion.13), channel_id=1, source_target_pairs={{0,16},{16,32},{32,48},{48,64},{64,80},{80,96},{96,112},{112,0},{1... | collective-permute-start | bytes 319496 | tf_op jit(solution)/shard_map/ppermute | solution.py:401
  187.3 0.7 copy-start.1

commit v3 on v2

--- a/solution.py
+++ b/solution.py
@@ -145,7 +145,7 @@
 
 
 def analysis_kernel(
-    order_ref, levels_ref, stape_ref, otape_ref, mine_ref, one_ref, two_ref, x_ref, mean_ref, obs_ref,
+    order_ref, levels_ref, stape_ref, otape_ref, mine_ref, one_ref, two_ref, x_ref, mean_ref, obs_ref, dep_ref,
     xo_ref, meano_ref, obso_ref, depo_ref,
     y_ref, d_ref, r_ref, c_ref, s_ref, u_ref, w_ref, a_ref, p_ref, v_ref, g_ref, dm_ref, do_ref, e_ref, x8_ref, low_ref, mid_ref, qr_ref, n_ref, k_ref, q_ref, part_ref, z_ref,
 ):
@@ -168,9 +168,8 @@
         for k in range(NB):
             line = one_ref[s, 32 + k : 33 + k, :B]
             d_ref[k, pl.ds(at, PIECE), :] = column(line, piece_eye)
-            var = column(line, var_eye)
-            r_ref[k, pl.ds(at, PIECE), :] = var
-            e_ref[k, pl.ds(at, PIECE), :] = jnp.sqrt(var)
+            r_ref[k, pl.ds(at, PIECE), :] = column(line, var_eye)
+            e_ref[k, pl.ds(at, PIECE), :] = column(jnp.sqrt(jnp.maximum(line, 0.0)), var_eye)
         return carry
 
     lax.fori_loop(0, ZS * CS, unpack, 0)
@@ -310,18 +309,18 @@
     for q in range(KB):
         sl = slice(q * PIECE, q * PIECE + PIECE)
         sub = jnp.sum(jnp.where(piece_eye, do_ref[sl, :], 0.0), axis=0, keepdims=True)
-        depo_ref[q : q + 1, :] = sub
-
-
-def analysis(order, levels, stape, otape, mine, one, two, x, mean, obs):
+        depo_ref[q : q + 1, :] = dep_ref[q : q + 1, :] - sub[:, :PIECE]
+
+
+def analysis(order, levels, stape, otape, mine, one, two, x, mean, obs, dep):
     shape = lambda *dims: jax.ShapeDtypeStruct(dims, F32)
     scratch = lambda *dims: pltpu.VMEM(dims, F32)
     vmem = pl.BlockSpec(memory_space=pltpu.VMEM)
     rows = x.shape[0]
     return pl.pallas_call(
         analysis_kernel,
-        out_shape=[shape(rows, M), shape(rows // B, B), shape(KB * PIECE, M), shape(KB, B)],
-        in_specs=[pl.BlockSpec(memory_space=pltpu.SMEM)] * 5 + [vmem] * 5,
+        out_shape=[shape(rows, M), shape(rows // B, B), shape(KB * PIECE, M), shape(KB, PIECE)],
+        in_specs=[pl.BlockSpec(memory_space=pltpu.SMEM)] * 5 + [vmem] * 6,
         out_specs=[vmem] * 4,
         scratch_shapes=[
             scratch(NB, N, M),
@@ -349,7 +348,7 @@
             scratch(N, WIDE),
         ],
         name="analysis",
-    )(order, levels, stape, otape, mine, one, two, x, mean, obs)
+    )(order, levels, stape, otape, mine, one, two, x, mean, obs, dep)
 
 
 ROWS = 104
@@ -396,11 +395,17 @@
     second = (row == 33) | ((row >= 48) & (row < 80))
     third = (row == 34) | ((row >= 40) & (row < 48)) | (row >= 80)
     far = jnp.where(second, away[1], jnp.where(third, away[2], away[0]))
-    step = size // 2
-    while step:
-        moved = lax.ppermute(block, axis, [(i, (i + step) % size) for i in range(size)])
-        block = jnp.where(far % (2 * step) == 0, block, moved)
-        step //= 2
+    rounds = {
+        4: [{1: (1,), -1: (3,), 2: (2,)}],
+        8: [{1: (1,), -1: (7,)}, {3: (2, 3, 4), -3: (5, 6)}],
+    }
+    for shifts in rounds[size]:
+        moved = {n: lax.ppermute(block, axis, [(i, (i + n) % size) for i in range(size)]) for n in shifts}
+        for n, reached in shifts.items():
+            take = far == reached[0]
+            for distance in reached[1:]:
+                take = take | (far == distance)
+            block = jnp.where(take, moved[n], block)
     return block
 
 
@@ -414,15 +419,15 @@
     two = lax.all_gather(payload[48:], ("z", "c"))
     mine = (shard * PIECE // B).astype(jnp.int32).reshape(1)
     rows = state_anom.shape[0]
-    anomaly, mean, obs_now, moved = analysis(
+    anomaly, mean, obs_now, depart = analysis(
         batch_order, taper_levels, state_taper, obs_taper, mine, one, two,
-        state_anom, state_mean.reshape(rows // B, B), obs_anom.reshape(KB * PIECE, M),
+        state_anom, state_mean.reshape(rows // B, B), obs_anom.reshape(KB * PIECE, M), obs_depart,
     )
     return (
         anomaly,
         mean.reshape(rows),
         obs_now.reshape(obs_anom.shape),
-        obs_depart - moved[:, :PIECE],
+        depart,
     )
 
 

time: 190 us -> 187 us (0.984)
  starting transfers between devices: 24.6 us -> 27.4 us
  waiting for transfers between devices: 10.6 us -> 8.1 us
    ppermute x5 -> x7, starting transfers between devices: 24.6 us -> 27.4 us  [spread(): lax.ppermute(block, axis, [(i, (i + n) % size) for i in range(size)])]
    ppermute x5 -> x7, waiting for transfers between devices: 10.6 us -> 8.1 us  [spread(): lax.ppermute(block, axis, [(i, (i + n) % size) for i in range(size)])]
  transfers between devices with their start and end apart: 5 -> 7, of which waited for: 4 -> 4; matrix products, arithmetic and copies ran while one was open for 1% -> 1% of each run, Pallas kernels for 0% -> 0%
where the time goes in v3:
time: 187 us
  Pallas kernels  95 us (51%)
  blocking collectives  49.8 us (27%)
  starting transfers between devices  27.4 us (15%)
  waiting for transfers between devices  8.1 us (4%)
  between operations  4.85 us (3%)
    pallas_call x1, Pallas kernels, analysis(): pl.pallas_call(analysis_kernel, out_shape=[shape(rows, M), shape(rows //...  92.9 us
    all_gather x1, blocking collectives, per_device(): one = lax.all_gather(payload[:48], ('z', 'c'))  31.3 us
    ppermute x7, starting transfers between devices, spread(): lax.ppermute(block, axis, [(i, (i + n) % size) for i in range(size)])  27.4 us
    all_gather x1, blocking collectives, per_device(): two = lax.all_gather(payload[48:], ('z', 'c'))  18.5 us
    ppermute x7, waiting for transfers between devices, spread(): lax.ppermute(block, axis, [(i, (i + n) % size) for i in range(size)])  8.1 us
  transfers between devices with their start and end apart: 7, of which 4 were waited for; matrix products, arithmetic and copies ran while one was open for 1% of the time, Pallas kernels for 0%

profile of v3, /device:TPU:1, one launch (start us, length us, event | category | flops | bytes accessed | tf_op | source)
XLA Modules:
  0.0 186.7 jit_solution(12818221262113423196)
XLA Ops:
  0.6 0.0 copy-start.1
  0.6 2.1 %prepare.1 = f32[104,256]{1,0:T(8,128)} custom-call(s32[3]{0:T(128)} %order_ref.3, f32[8]{0:T(128)} %levels_ref.3, s32[8,256]{1,0:T(8,128)} %otape_ref.3, f32[2,32,256]{2,1,0:T(8,128)} %obs_ref.1, f32[2,32]{1,0:T(2,128)} %dep_ref.3, f32[2,32]{1,0:T(2,128)} %var_ref.1), custom_call_target="tpu_custom_call" | custom-call | tf_op jit(solution)/shard_map/prepare/pallas_call | solution.py:382
  2.7 0.0 copy-start
  2.7 4.1 %collective-permute-start.2 = (f32[104,256]{1,0:T(8,128)}, f32[104,256]{1,0:T(8,128)S(1)}, u32[]{:S(2)}, u32[]{:S(2)}) collective-permute-start(f32[104,256]{1,0:T(8,128)} %prepare.1), channel_id=1, source_target_pairs={{0,128},{128,256},{256,384},{384,0},{1,129},{129,257},{257,385},{3... | collective-permute-start | bytes 319496 | tf_op jit(solution)/shard_map/ppermute | solution.py:403
  6.8 3.2 %collective-permute-start.1 = (f32[104,256]{1,0:T(8,128)}, f32[104,256]{1,0:T(8,128)S(1)}, u32[]{:S(2)}, u32[]{:S(2)}) collective-permute-start(f32[104,256]{1,0:T(8,128)} %prepare.1), channel_id=1, source_target_pairs={{0,384},{128,0},{256,128},{384,256},{1,385},{129,1},{257,129},{385... | collective-permute-start | bytes 319496 | tf_op jit(solution)/shard_map/ppermute | solution.py:403
  10.0 3.6 %collective-permute-start = (f32[104,256]{1,0:T(8,128)}, f32[104,256]{1,0:T(8,128)S(1)}, u32[]{:S(2)}, u32[]{:S(2)}) collective-permute-start(f32[104,256]{1,0:T(8,128)} %prepare.1), channel_id=1, source_target_pairs={{0,256},{128,384},{256,0},{384,128},{1,257},{129,385},{257,1},{385... | collective-permute-start | bytes 319496 | tf_op jit(solution)/shard_map/ppermute | solution.py:403
  13.6 0.0 copy-done.1
  13.7 0.6 fusion.4
  16.2 0.6 fusion.3
  18.9 0.0 collective-permute-done.2
  18.9 0.0 collective-permute-done.1
  18.9 0.0 collective-permute-done
  18.9 0.0 copy-done
  18.9 0.1 select_select_fusion.2
  19.0 3.2 %collective-permute-start.4 = (f32[104,256]{1,0:T(8,128)S(1)}, f32[104,256]{1,0:T(8,128)S(1)}, u32[]{:S(2)}, u32[]{:S(2)}) collective-permute-start(f32[104,256]{1,0:T(8,128)S(1)} %select_select_fusion.2), channel_id=1, source_target_pairs={{0,16},{16,32},{32,48},{48,64},{64,80},{80,96},{96,112},{112,0},{1... | collective-permute-start | bytes 319496 | tf_op jit(solution)/shard_map/ppermute | solution.py:403
  22.2 3.8 %collective-permute-start.3 = (f32[104,256]{1,0:T(8,128)S(1)}, f32[104,256]{1,0:T(8,128)S(1)}, u32[]{:S(2)}, u32[]{:S(2)}) collective-permute-start(f32[104,256]{1,0:T(8,128)S(1)} %select_select_fusion.2), channel_id=1, source_target_pairs={{0,112},{16,0},{32,16},{48,32},{64,48},{80,64},{96,80},{112,96},{1... | collective-permute-start | bytes 319496 | tf_op jit(solution)/shard_map/ppermute | solution.py:403
  26.1 0.1 collective-permute-done.4
  26.2 1.5 collective-permute-done.3
  27.7 0.1 select_select_fusion.1
  27.9 7.6 %collective-permute-start.6 = (f32[104,256]{1,0:T(8,128)S(1)}, f32[104,256]{1,0:T(8,128)S(1)}, u32[]{:S(2)}, u32[]{:S(2)}) collective-permute-start(f32[104,256]{1,0:T(8,128)S(1)} %select_select_fusion.1), channel_id=1, source_target_pairs={{0,48},{16,64},{32,80},{48,96},{64,112},{80,0},{96,16},{112,32},{1... | collective-permute-start | bytes 319496 | tf_op jit(solution)/shard_map/ppermute | solution.py:403
  35.4 1.9 %collective-permute-start.5 = (f32[104,256]{1,0:T(8,128)S(1)}, f32[104,256]{1,0:T(8,128)S(1)}, u32[]{:S(2)}, u32[]{:S(2)}) collective-permute-start(f32[104,256]{1,0:T(8,128)S(1)} %select_select_fusion.1), channel_id=1, source_target_pairs={{0,80},{16,96},{32,112},{48,0},{64,16},{80,32},{96,48},{112,64},{1... | collective-permute-start | bytes 319496 | tf_op jit(solution)/shard_map/ppermute | solution.py:403
  37.4 1.6 collective-permute-done.6
  39.0 4.8 %collective-permute-done.5 = f32[104,256]{1,0:T(8,128)S(1)} collective-permute-done((f32[104,256]{1,0:T(8,128)S(1)}, f32[104,256]{1,0:T(8,128)S(1)}, u32[]{:S(2)}, u32[]{:S(2)}) %collective-permute-start.5) | collective-permute-done | bytes 106528 | tf_op jit(solution)/shard_map/ppermute | solution.py:403
  43.8 0.1 select_select_fusion
  44.0 31.3 %all-gather = f32[768,256]{1,0:T(8,128)} all-gather(f32[48,256]{1,0:T(8,128)S(1)} %slice.32), channel_id=2, replica_groups=mesh['x'=4,'y'=8,'z'=8,'c'=2] {'z','c'}, dimensions={0}, use_global_device_ids=true | all-gather | bytes 835584 | tf_op jit(solution)/shard_map/all_gather | solution.py:418
  75.3 18.5 %all-gather.1 = f32[896,256]{1,0:T(8,128)} all-gather(f32[56,256]{1,0:T(8,128)S(1)} %slice.33), channel_id=3, replica_groups=mesh['x'=4,'y'=8,'z'=8,'c'=2] {'z','c'}, dimensions={0}, use_global_device_ids=true | all-gather | bytes 974848 | tf_op jit(solution)/shard_map/all_gather | solution.py:419
  93.8 92.9 %analysis.1 = (f32[1024,256]{1,0:T(8,128)}, f32[8,128]{1,0:T(8,128)}, f32[64,256]{1,0:T(8,128)}, f32[2,32]{1,0:T(2,128)}) custom-call(s32[3]{0:T(128)} %order_ref.3, f32[8]{0:T(128)} %levels_ref.3, s32[8,256]{1,0:T(8,128)} %stape_ref.1, s32[8,256]{1,0:T(8,128)} %otape_ref.3, s32[1]{0:T(128)} %bitcast.mine_ref, f32[16,48,256]{2,1,0:T(8,128)} %bitcast.14, ...), custom_call_target="tpu_custom_call" | custom-call | tf_op jit(solution)/shard_map/analysis/pallas_call | solution.py:320
  (7 shorter events, 0.1 us)
Async XLA Ops:
  0.6 13.0 %copy-start.1 = (s32[3]{0:T(128)S(1)}, s32[3]{0:T(128)}, u32[]{:S(2)}) copy-start(s32[3]{0:T(128)} %order_ref.3) | copy-start | bytes 40
  2.7 16.2 %copy-start = (f32[104,256]{1,0:T(8,128)S(1)}, f32[104,256]{1,0:T(8,128)}, u32[]{:S(2)}) copy-start(f32[104,256]{1,0:T(8,128)} %prepare.1) | copy-start | bytes 319492
  2.7 16.2 %collective-permute-start.2 = (f32[104,256]{1,0:T(8,128)}, f32[104,256]{1,0:T(8,128)S(1)}, u32[]{:S(2)}, u32[]{:S(2)}) collective-permute-start(f32[104,256]{1,0:T(8,128)} %prepare.1), channel_id=1, source_target_pairs={{0,128},{128,256},{256,384},{384,0},{1,129},{129,257},{257,385},{3... | collective-permute-start | bytes 319496 | tf_op jit(solution)/shard_map/ppermute | solution.py:403
  6.8 12.1 %collective-permute-start.1 = (f32[104,256]{1,0:T(8,128)}, f32[104,256]{1,0:T(8,128)S(1)}, u32[]{:S(2)}, u32[]{:S(2)}) collective-permute-start(f32[104,256]{1,0:T(8,128)} %prepare.1), channel_id=1, source_target_pairs={{0,384},{128,0},{256,128},{384,256},{1,385},{129,1},{257,129},{385... | collective-permute-start | bytes 319496 | tf_op jit(solution)/shard_map/ppermute | solution.py:403
  10.0 8.9 %collective-permute-start = (f32[104,256]{1,0:T(8,128)}, f32[104,256]{1,0:T(8,128)S(1)}, u32[]{:S(2)}, u32[]{:S(2)}) collective-permute-start(f32[104,256]{1,0:T(8,128)} %prepare.1), channel_id=1, source_target_pairs={{0,256},{128,384},{256,0},{384,128},{1,257},{129,385},{257,1},{385... | collective-permute-start | bytes 319496 | tf_op jit(solution)/shard_map/ppermute | solution.py:403
  19.0 7.2 %collective-permute-start.4 = (f32[104,256]{1,0:T(8,128)S(1)}, f32[104,256]{1,0:T(8,128)S(1)}, u32[]{:S(2)}, u32[]{:S(2)}) collective-permute-start(f32[104,256]{1,0:T(8,128)S(1)} %select_select_fusion.2), channel_id=1, source_target_pairs={{0,16},{16,32},{32,48},{48,64},{64,80},{80,96},{96,112},{112,0},{1... | collective-permute-start | bytes 319496 | tf_op jit(solution)/shard_map/ppermute | solution.py:403
  22.2 5.5 %collective-permute-start.3 = (f32[104,256]{1,0:T(8,128)S(1)}, f32[104,256]{1,0:T(8,128)S(1)}, u32[]{:S(2)}, u32[]{:S(2)}) collective-permute-start(f32[104,256]{1,0:T(8,128)S(1)} %select_select_fusion.2), channel_id=1, source_target_pairs={{0,112},{16,0},{32,16},{48,32},{64,48},{80,64},{96,80},{112,96},{1... | collective-permute-start | bytes 319496 | tf_op jit(solution)/shard_map/ppermute | solution.py:403
  27.9 11.2 %collective-permute-start.6 = (f32[104,256]{1,0:T(8,128)S(1)}, f32[104,256]{1,0:T(8,128)S(1)}, u32[]{:S(2)}, u32[]{:S(2)}) collective-permute-start(f32[104,256]{1,0:T(8,128)S(1)} %select_select_fusion.1), channel_id=1, source_target_pairs={{0,48},{16,64},{32,80},{48,96},{64,112},{80,0},{96,16},{112,32},{1... | collective-permute-start | bytes 319496 | tf_op jit(solution)/shard_map/ppermute | solution.py:403
  35.4 8.4 %collective-permute-start.5 = (f32[104,256]{1,0:T(8,128)S(1)}, f32[104,256]{1,0:T(8,128)S(1)}, u32[]{:S(2)}, u32[]{:S(2)}) collective-permute-start(f32[104,256]{1,0:T(8,128)S(1)} %select_select_fusion.1), channel_id=1, source_target_pairs={{0,80},{16,96},{32,112},{48,0},{64,16},{80,32},{96,48},{112,64},{1... | collective-permute-start | bytes 319496 | tf_op jit(solution)/shard_map/ppermute | solution.py:403

commit v4 on v3

--- a/solution.py
+++ b/solution.py
@@ -172,7 +172,7 @@
             e_ref[k, pl.ds(at, PIECE), :] = column(jnp.sqrt(jnp.maximum(line, 0.0)), var_eye)
         return carry
 
-    lax.fori_loop(0, ZS * CS, unpack, 0)
+    lax.fori_loop(0, ZS * CS, unpack, 0, unroll=8)
     for k in range(NB):
         c_ref[k * pairs : k * pairs + pairs, :] = column(one_ref[0, 32 + k : 33 + k, :B], pair_eye)
     xo_ref[...] = x_ref[...]
@@ -281,21 +281,21 @@
             line = jnp.sum(y_ref[k, sl, :] * wide(z_ref[sl, M:]), axis=0, keepdims=True)
             qr_ref[slot, b : b + 1, :] = line * (1.0 / (M - 1))
 
-        def cross_step(n, carry):
-            later, i = n // NBLK, n % NBLK
-            at = pl.multiple_of(i * B, B)
-
-            def weight(j):
-                line = c_ref[pl.ds(later * pairs + k * (NBLK * NBLK) + i * NBLK + j, 1), :]
-                return jnp.concatenate([line] * (M // B), axis=1)
-
-            rows = y_ref[later, pl.ds(at, B), :]
-            delta, move = update(rows, slot, weight)
-            y_ref[later, pl.ds(at, B), :] = rows - delta
-            d_ref[later, pl.ds(at, B), :] = d_ref[later, pl.ds(at, B), :] - move
+        def cross_step(later, carry):
+            for i in range(NBLK):
+                sl = slice(i * B, i * B + B)
+
+                def weight(j):
+                    line = c_ref[pl.ds(later * pairs + k * (NBLK * NBLK) + i * NBLK + j, 1), :]
+                    return wide(line)
+
+                rows = y_ref[later, sl, :]
+                delta, move = update(rows, slot, weight)
+                y_ref[later, sl, :] = rows - delta
+                d_ref[later, sl, :] = d_ref[later, sl, :] - move
             return carry
 
-        lax.fori_loop((k + 1) * NBLK, NB * NBLK, cross_step, 0)
+        lax.fori_loop(k + 1, NB, cross_step, 0)
         return outer
 
     lax.fori_loop(0, NB, batch_step, 0)

time: 187 us -> 185 us (0.989)
  Pallas kernels: 95 us -> 92.8 us
    pallas_call x1, Pallas kernels: 92.9 us -> 90.8 us  [analysis(): pl.pallas_call(analysis_kernel, out_shape=[shape(rows, M), shape(rows //...]
where the time goes in v4:
time: 185 us
  Pallas kernels  92.8 us (50%)
  blocking collectives  49.8 us (27%)
  starting transfers between devices  27.4 us (15%)
  waiting for transfers between devices  8.1 us (4%)
  between operations  4.85 us (3%)
    pallas_call x1, Pallas kernels, analysis(): pl.pallas_call(analysis_kernel, out_shape=[shape(rows, M), shape(rows //...  90.8 us
    all_gather x1, blocking collectives, per_device(): one = lax.all_gather(payload[:48], ('z', 'c'))  31.3 us
    ppermute x7, starting transfers between devices, spread(): lax.ppermute(block, axis, [(i, (i + n) % size) for i in range(size)])  27.4 us
    all_gather x1, blocking collectives, per_device(): two = lax.all_gather(payload[48:], ('z', 'c'))  18.5 us
    ppermute x7, waiting for transfers between devices, spread(): lax.ppermute(block, axis, [(i, (i + n) % size) for i in range(size)])  8.1 us
  transfers between devices with their start and end apart: 7, of which 4 were waited for; matrix products, arithmetic and copies ran while one was open for 1% of the time, Pallas kernels for 0%

profile of v4, /device:TPU:1, one launch (start us, length us, event | category | flops | bytes accessed | tf_op | source)
XLA Modules:
  0.0 184.5 jit_solution(15013599053586742597)
XLA Ops:
  0.6 0.0 copy-start.1
  0.6 2.1 %prepare.1 = f32[104,256]{1,0:T(8,128)} custom-call(s32[3]{0:T(128)} %order_ref.3, f32[8]{0:T(128)} %levels_ref.3, s32[8,256]{1,0:T(8,128)} %otape_ref.3, f32[2,32,256]{2,1,0:T(8,128)} %obs_ref.1, f32[2,32]{1,0:T(2,128)} %dep_ref.3, f32[2,32]{1,0:T(2,128)} %var_ref.1), custom_call_target="tpu_custom_call" | custom-call | tf_op jit(solution)/shard_map/prepare/pallas_call | solution.py:382
  2.7 0.0 copy-start
  2.7 4.1 %collective-permute-start.2 = (f32[104,256]{1,0:T(8,128)}, f32[104,256]{1,0:T(8,128)S(1)}, u32[]{:S(2)}, u32[]{:S(2)}) collective-permute-start(f32[104,256]{1,0:T(8,128)} %prepare.1), channel_id=1, source_target_pairs={{0,128},{128,256},{256,384},{384,0},{1,129},{129,257},{257,385},{3... | collective-permute-start | bytes 319496 | tf_op jit(solution)/shard_map/ppermute | solution.py:403
  6.8 3.2 %collective-permute-start.1 = (f32[104,256]{1,0:T(8,128)}, f32[104,256]{1,0:T(8,128)S(1)}, u32[]{:S(2)}, u32[]{:S(2)}) collective-permute-start(f32[104,256]{1,0:T(8,128)} %prepare.1), channel_id=1, source_target_pairs={{0,384},{128,0},{256,128},{384,256},{1,385},{129,1},{257,129},{385... | collective-permute-start | bytes 319496 | tf_op jit(solution)/shard_map/ppermute | solution.py:403
  10.0 3.6 %collective-permute-start = (f32[104,256]{1,0:T(8,128)}, f32[104,256]{1,0:T(8,128)S(1)}, u32[]{:S(2)}, u32[]{:S(2)}) collective-permute-start(f32[104,256]{1,0:T(8,128)} %prepare.1), channel_id=1, source_target_pairs={{0,256},{128,384},{256,0},{384,128},{1,257},{129,385},{257,1},{385... | collective-permute-start | bytes 319496 | tf_op jit(solution)/shard_map/ppermute | solution.py:403
  13.6 0.0 copy-done.1
  13.7 0.6 fusion.4
  16.2 0.6 fusion.3
  18.9 0.0 collective-permute-done.2
  18.9 0.0 collective-permute-done.1
  18.9 0.0 collective-permute-done
  18.9 0.0 copy-done
  18.9 0.1 select_select_fusion.2
  19.0 3.2 %collective-permute-start.4 = (f32[104,256]{1,0:T(8,128)S(1)}, f32[104,256]{1,0:T(8,128)S(1)}, u32[]{:S(2)}, u32[]{:S(2)}) collective-permute-start(f32[104,256]{1,0:T(8,128)S(1)} %select_select_fusion.2), channel_id=1, source_target_pairs={{0,16},{16,32},{32,48},{48,64},{64,80},{80,96},{96,112},{112,0},{1... | collective-permute-start | bytes 319496 | tf_op jit(solution)/shard_map/ppermute | solution.py:403
  22.2 3.8 %collective-permute-start.3 = (f32[104,256]{1,0:T(8,128)S(1)}, f32[104,256]{1,0:T(8,128)S(1)}, u32[]{:S(2)}, u32[]{:S(2)}) collective-permute-start(f32[104,256]{1,0:T(8,128)S(1)} %select_select_fusion.2), channel_id=1, source_target_pairs={{0,112},{16,0},{32,16},{48,32},{64,48},{80,64},{96,80},{112,96},{1... | collective-permute-start | bytes 319496 | tf_op jit(solution)/shard_map/ppermute | solution.py:403
  26.1 0.1 collective-permute-done.4
  26.2 1.5 collective-permute-done.3
  27.7 0.1 select_select_fusion.1
  27.9 7.6 %collective-permute-start.6 = (f32[104,256]{1,0:T(8,128)S(1)}, f32[104,256]{1,0:T(8,128)S(1)}, u32[]{:S(2)}, u32[]{:S(2)}) collective-permute-start(f32[104,256]{1,0:T(8,128)S(1)} %select_select_fusion.1), channel_id=1, source_target_pairs={{0,48},{16,64},{32,80},{48,96},{64,112},{80,0},{96,16},{112,32},{1... | collective-permute-start | bytes 319496 | tf_op jit(solution)/shard_map/ppermute | solution.py:403
  35.4 1.9 %collective-permute-start.5 = (f32[104,256]{1,0:T(8,128)S(1)}, f32[104,256]{1,0:T(8,128)S(1)}, u32[]{:S(2)}, u32[]{:S(2)}) collective-permute-start(f32[104,256]{1,0:T(8,128)S(1)} %select_select_fusion.1), channel_id=1, source_target_pairs={{0,80},{16,96},{32,112},{48,0},{64,16},{80,32},{96,48},{112,64},{1... | collective-permute-start | bytes 319496 | tf_op jit(solution)/shard_map/ppermute | solution.py:403
  37.4 1.6 collective-permute-done.6
  39.0 4.8 %collective-permute-done.5 = f32[104,256]{1,0:T(8,128)S(1)} collective-permute-done((f32[104,256]{1,0:T(8,128)S(1)}, f32[104,256]{1,0:T(8,128)S(1)}, u32[]{:S(2)}, u32[]{:S(2)}) %collective-permute-start.5) | collective-permute-done | bytes 106528 | tf_op jit(solution)/shard_map/ppermute | solution.py:403
  43.8 0.1 select_select_fusion
  44.0 31.3 %all-gather = f32[768,256]{1,0:T(8,128)} all-gather(f32[48,256]{1,0:T(8,128)S(1)} %slice.32), channel_id=2, replica_groups=mesh['x'=4,'y'=8,'z'=8,'c'=2] {'z','c'}, dimensions={0}, use_global_device_ids=true | all-gather | bytes 835584 | tf_op jit(solution)/shard_map/all_gather | solution.py:418
  75.3 18.5 %all-gather.1 = f32[896,256]{1,0:T(8,128)} all-gather(f32[56,256]{1,0:T(8,128)S(1)} %slice.33), channel_id=3, replica_groups=mesh['x'=4,'y'=8,'z'=8,'c'=2] {'z','c'}, dimensions={0}, use_global_device_ids=true | all-gather | bytes 974848 | tf_op jit(solution)/shard_map/all_gather | solution.py:419
  93.8 90.8 %analysis.1 = (f32[1024,256]{1,0:T(8,128)}, f32[8,128]{1,0:T(8,128)}, f32[64,256]{1,0:T(8,128)}, f32[2,32]{1,0:T(2,128)}) custom-call(s32[3]{0:T(128)} %order_ref.3, f32[8]{0:T(128)} %levels_ref.3, s32[8,256]{1,0:T(8,128)} %stape_ref.1, s32[8,256]{1,0:T(8,128)} %otape_ref.3, s32[1]{0:T(128)} %bitcast.mine_ref, f32[16,48,256]{2,1,0:T(8,128)} %bitcast.14, ...), custom_call_target="tpu_custom_call" | custom-call | tf_op jit(solution)/shard_map/analysis/pallas_call | solution.py:320
  (7 shorter events, 0.1 us)
Async XLA Ops:
  0.6 13.0 %copy-start.1 = (s32[3]{0:T(128)S(1)}, s32[3]{0:T(128)}, u32[]{:S(2)}) copy-start(s32[3]{0:T(128)} %order_ref.3) | copy-start | bytes 40
  2.7 16.2 %copy-start = (f32[104,256]{1,0:T(8,128)S(1)}, f32[104,256]{1,0:T(8,128)}, u32[]{:S(2)}) copy-start(f32[104,256]{1,0:T(8,128)} %prepare.1) | copy-start | bytes 319492
  2.7 16.2 %collective-permute-start.2 = (f32[104,256]{1,0:T(8,128)}, f32[104,256]{1,0:T(8,128)S(1)}, u32[]{:S(2)}, u32[]{:S(2)}) collective-permute-start(f32[104,256]{1,0:T(8,128)} %prepare.1), channel_id=1, source_target_pairs={{0,128},{128,256},{256,384},{384,0},{1,129},{129,257},{257,385},{3... | collective-permute-start | bytes 319496 | tf_op jit(solution)/shard_map/ppermute | solution.py:403
  6.8 12.1 %collective-permute-start.1 = (f32[104,256]{1,0:T(8,128)}, f32[104,256]{1,0:T(8,128)S(1)}, u32[]{:S(2)}, u32[]{:S(2)}) collective-permute-start(f32[104,256]{1,0:T(8,128)} %prepare.1), channel_id=1, source_target_pairs={{0,384},{128,0},{256,128},{384,256},{1,385},{129,1},{257,129},{385... | collective-permute-start | bytes 319496 | tf_op jit(solution)/shard_map/ppermute | solution.py:403
  10.0 8.9 %collective-permute-start = (f32[104,256]{1,0:T(8,128)}, f32[104,256]{1,0:T(8,128)S(1)}, u32[]{:S(2)}, u32[]{:S(2)}) collective-permute-start(f32[104,256]{1,0:T(8,128)} %prepare.1), channel_id=1, source_target_pairs={{0,256},{128,384},{256,0},{384,128},{1,257},{129,385},{257,1},{385... | collective-permute-start | bytes 319496 | tf_op jit(solution)/shard_map/ppermute | solution.py:403
  19.0 7.2 %collective-permute-start.4 = (f32[104,256]{1,0:T(8,128)S(1)}, f32[104,256]{1,0:T(8,128)S(1)}, u32[]{:S(2)}, u32[]{:S(2)}) collective-permute-start(f32[104,256]{1,0:T(8,128)S(1)} %select_select_fusion.2), channel_id=1, source_target_pairs={{0,16},{16,32},{32,48},{48,64},{64,80},{80,96},{96,112},{112,0},{1... | collective-permute-start | bytes 319496 | tf_op jit(solution)/shard_map/ppermute | solution.py:403
  22.2 5.5 %collective-permute-start.3 = (f32[104,256]{1,0:T(8,128)S(1)}, f32[104,256]{1,0:T(8,128)S(1)}, u32[]{:S(2)}, u32[]{:S(2)}) collective-permute-start(f32[104,256]{1,0:T(8,128)S(1)} %select_select_fusion.2), channel_id=1, source_target_pairs={{0,112},{16,0},{32,16},{48,32},{64,48},{80,64},{96,80},{112,96},{1... | collective-permute-start | bytes 319496 | tf_op jit(solution)/shard_map/ppermute | solution.py:403
  27.9 11.2 %collective-permute-start.6 = (f32[104,256]{1,0:T(8,128)S(1)}, f32[104,256]{1,0:T(8,128)S(1)}, u32[]{:S(2)}, u32[]{:S(2)}) collective-permute-start(f32[104,256]{1,0:T(8,128)S(1)} %select_select_fusion.1), channel_id=1, source_target_pairs={{0,48},{16,64},{32,80},{48,96},{64,112},{80,0},{96,16},{112,32},{1... | collective-permute-start | bytes 319496 | tf_op jit(solution)/shard_map/ppermute | solution.py:403
  35.4 8.4 %collective-permute-start.5 = (f32[104,256]{1,0:T(8,128)S(1)}, f32[104,256]{1,0:T(8,128)S(1)}, u32[]{:S(2)}, u32[]{:S(2)}) collective-permute-start(f32[104,256]{1,0:T(8,128)S(1)} %select_select_fusion.1), channel_id=1, source_target_pairs={{0,80},{16,96},{32,112},{48,0},{64,16},{80,32},{96,48},{112,64},{1... | collective-permute-start | bytes 319496 | tf_op jit(solution)/shard_map/ppermute | solution.py:403
